TPU v7x, 128 devices: a whole 4x4x4 slice. The times are simulated.
128 devices in a mesh: rep: 4 (over y_hi, core), fsdp: 32 (over x, z, y_lo).
Axes of the slice: x: 4, y: 4 (y_hi: 2, y_lo: 2; y = y_hi * 2 + y_lo), z: 4, core: 2. Of those that a mesh axis runs over, the one named last changes fastest.
Arguments:
- query_rows: bfloat16 [4, 12288, 2560], P('rep', 'fsdp'), may hold values from -5 to 5
- key_rows: bfloat16 [4, 12288, 2560], P('rep', 'fsdp'), may hold values from -5 to 5
- value_rows: bfloat16 [4, 12288, 2560], P('rep', 'fsdp'), may hold values from -5 to 5
- residual_in: bfloat16 [4, 12288, 2560], P('rep', 'fsdp'), may hold values from -6 to 6
- out_grad: bfloat16 [4, 12288, 2560], P('rep', 'fsdp'), may hold values from -6 to 6
- doc_ids: int32 [4, 12288], P('rep', 'fsdp'), may hold values from 0 to 191, never falling along the last dimension, each value on 1 to 256 neighbouring positions
- out_weight: bfloat16 [4, 2560, 2560], P('rep', 'fsdp'), may hold values from -0.125 to 0.125
- momentum: float32 [4, 2560, 2560], P('rep', 'fsdp'), may hold values from -192 to 192
- step_index: int32 [1], replicated, may hold values from 0 to 63
Outputs:
- block_out: bfloat16 [4, 12288, 2560], P('rep', 'fsdp')
- query_grad: bfloat16 [4, 12288, 2560], P('rep', 'fsdp')
- key_grad: bfloat16 [4, 12288, 2560], P('rep', 'fsdp')
- value_grad: bfloat16 [4, 12288, 2560], P('rep', 'fsdp')
- new_weight: bfloat16 [4, 2560, 2560], P('rep', 'fsdp')
- new_momentum: float32 [4, 2560, 2560], P('rep', 'fsdp')
All inputs are finite; a program needn't handle non-finite values.
Results may differ from a plain program's by a relative error of at most 0.018.
Values may be sent and summed in bfloat16 or wider, within the bound.
No kernel may reach another device: no remote copies, remote signals or barrier semaphores. Data moves between devices by JAX's collectives and lax.ppermute only.
A program may use at most 192 MiB of HBM per device.

v0:
```python
import functools

import jax
import jax.numpy as jnp
from jax import lax
from jax.sharding import Mesh
from jax.sharding import PartitionSpec as P

HEADS = 20
HEAD_SIZE = 128
FSDP = ("fsdp_0", "fsdp_1", "fsdp_2")


momentum_decay = 0.9
learning_rate = 0.0003


def as_sent(shard):
    return jax.tree.map(lambda a: a.astype(jnp.bfloat16) if a.dtype == jnp.float32 else a, shard)


def swapped(block, axis, distance):
    count = lax.axis_size(axis)
    route = []
    for low in range(count):
        high = low | 1 << distance
        if high != low and high < count:
            route += [(low, high), (high, low)]
    return lax.ppermute(block, axis, route)


def piece_ends(length, count):
    unit = 8 if length >= 8 * count else 1
    return [length // unit * k // count * unit for k in range(1, count)]


def stacked_from(shard, axes, order):
    tiles = shard
    for k in order:
        tiles = lax.all_gather(tiles, axes[k])
    done = order[::-1]
    back = [done.index(k) for k in range(len(axes))]
    tiles = tiles.transpose(*back, *range(len(axes), tiles.ndim))
    return tiles.reshape(-1, *shard.shape)


def in_order(tiles, dim):
    shape = list(tiles.shape[1:])
    shape[dim] *= tiles.shape[0]
    return jnp.moveaxis(tiles, 0, dim).reshape(shape)


def gather_at_once(shard, axes, dim):
    cut = max(range(max(1, shard.ndim - 1)), key=lambda d: shard.shape[d])
    count, done = (len(axes), [])
    for first, section in enumerate(
        jnp.split(shard, piece_ends(shard.shape[cut], count), axis=cut)
    ):
        if section.size:
            order = [(first - k) % count for k in range(count)]
            done.append(stacked_from(section, axes, order))
    return in_order(jnp.concatenate(done, axis=cut + 1), dim)


def attend_local(query_block, key_block, value_block, doc_block):
    length = query_block.shape[0]
    heads = HEADS
    score_scale = HEAD_SIZE ** (-0.5)
    query_heads = query_block.reshape(length, heads, HEAD_SIZE)
    key_heads = key_block.reshape(length, heads, HEAD_SIZE)
    value_heads = value_block.reshape(length, heads, HEAD_SIZE)
    scores = (
        jnp.einsum("qhd,khd->hqk", query_heads, key_heads, preferred_element_type=jnp.float32)
        * score_scale
    )
    places = jnp.arange(length, dtype=jnp.int32)
    allowed = (places[None, :] <= places[:, None]) & (doc_block[:, None] == doc_block[None, :])
    scores = jnp.where(allowed[None], scores, -jnp.inf)
    row_peaks = jnp.max(scores, axis=-1, keepdims=True)
    exponents = jnp.exp(scores - row_peaks)
    attn_probs = exponents / jnp.sum(exponents, axis=-1, keepdims=True)
    probs_low = attn_probs.astype(jnp.bfloat16)
    context = jnp.einsum("hqk,khd->qhd", probs_low, value_heads, preferred_element_type=jnp.float32)
    context = context.reshape(length, heads * HEAD_SIZE).astype(jnp.bfloat16)
    return (context, attn_probs, probs_low, query_heads, key_heads, value_heads)


def attend_local_back(context_grad, attn_probs, probs_low, query_heads, key_heads, value_heads):
    length = query_heads.shape[0]
    width = HEADS * HEAD_SIZE
    score_scale = HEAD_SIZE ** (-0.5)
    grad_heads = context_grad.reshape(length, HEADS, HEAD_SIZE)
    value_grad = jnp.einsum(
        "hqk,qhd->khd", probs_low, grad_heads, preferred_element_type=jnp.float32
    )
    prob_grad = jnp.einsum(
        "qhd,khd->hqk", grad_heads, value_heads, preferred_element_type=jnp.float32
    )
    row_delta = jnp.sum(prob_grad * attn_probs, axis=-1, keepdims=True)
    score_grad = (attn_probs * (prob_grad - row_delta) * score_scale).astype(jnp.bfloat16)
    query_grad = jnp.einsum(
        "hqk,khd->qhd", score_grad, key_heads, preferred_element_type=jnp.float32
    )
    key_grad = jnp.einsum(
        "hqk,qhd->khd", score_grad, query_heads, preferred_element_type=jnp.float32
    )
    return (
        query_grad.reshape(length, width).astype(jnp.bfloat16),
        key_grad.reshape(length, width).astype(jnp.bfloat16),
        value_grad.reshape(length, width).astype(jnp.bfloat16),
    )


def partner_at(level, weights):
    return jax.tree.map(
        lambda part, own: part.astype(own.dtype), swapped(as_sent(weights), "rep", level), weights
    )


def on_device(
    query_rows,
    key_rows,
    value_rows,
    residual_in,
    out_grad,
    doc_ids,
    out_weight,
    momentum,
    step_index,
):
    context, attn_probs, probs_low, query_heads, key_heads, value_heads = attend_local(
        query_rows[0], key_rows[0], value_rows[0], doc_ids[0]
    )
    weight_shard = out_weight[0]
    grad_local = out_grad[0]
    gathered = gather_at_once(weight_shard, FSDP, 0)
    projected = jnp.dot(context, gathered, preferred_element_type=jnp.float32)
    context_grad = lax.dot_general(
        grad_local, gathered, (((1,), (1,)), ((), ())), preferred_element_type=jnp.float32
    )
    block_out = (residual_in[0].astype(jnp.float32) + projected).astype(jnp.bfloat16)
    context_grad = context_grad.astype(jnp.bfloat16)
    query_grad, key_grad, value_grad = attend_local_back(
        context_grad, attn_probs, probs_low, query_heads, key_heads, value_heads
    )
    weight_grad = lax.psum_scatter(
        lax.dot_general(
            context, grad_local, (((0,), (0,)), ((), ())), preferred_element_type=jnp.float32
        ).astype(jnp.bfloat16),
        FSDP,
        scatter_dimension=0,
        tiled=True,
    ).astype(jnp.float32)
    new_momentum = momentum_decay * momentum[0] + weight_grad
    stepped = (weight_shard.astype(jnp.float32) - learning_rate * new_momentum).astype(jnp.bfloat16)
    levels = lax.axis_size("rep").bit_length() - 1
    chosen_level = step_index[0] % levels
    branches = [functools.partial(partner_at, level) for level in range(levels)]
    partner = lax.switch(chosen_level, branches, stepped)
    new_weight = ((stepped.astype(jnp.float32) + partner.astype(jnp.float32)) * 0.5).astype(
        jnp.bfloat16
    )
    return (
        block_out[None],
        query_grad[None],
        key_grad[None],
        value_grad[None],
        new_weight[None],
        new_momentum[None],
    )


def solution(mesh):
    torus = Mesh(
        mesh.devices.reshape(mesh.shape["rep"], 4, 4, 2), ("rep", "fsdp_0", "fsdp_1", "fsdp_2")
    )
    return jax.shard_map(
        on_device,
        mesh=torus,
        in_specs=(
            P("rep", FSDP, None),
            P("rep", FSDP, None),
            P("rep", FSDP, None),
            P("rep", FSDP, None),
            P("rep", FSDP, None),
            P("rep", FSDP),
            P("rep", FSDP, None),
            P("rep", FSDP, None),
            P(),
        ),
        out_specs=(
            P("rep", FSDP, None),
            P("rep", FSDP, None),
            P("rep", FSDP, None),
            P("rep", FSDP, None),
            P("rep", FSDP, None),
            P("rep", FSDP, None),
        ),
        check_vma=False,
    )
```

profile of v0, /device:TPU:1, one launch (start us, length us, event | category | flops | bytes accessed | tf_op | source)
XLA Modules:
  0.0 455.6 jit_solution(11345548736362835934)
XLA Ops:
  8.0 0.0 all-gather.14.cloned.1.call-start
  8.1 1.1 fusion.47
  9.2 13.9 %all_gather.53 = bf16[4,24,2560]{2,1,0:T(8,128)(2,1)} all-gather(bf16[1,24,2560]{2,1,0:T(8,128)(2,1)S(1)} %get-tuple-element.44), channel_id=1, replica_groups=mesh['rep'=4,'fsdp_0'=4,'fsdp_1'=4,'fsdp_2'=2] {'fsdp_1'}, dimensions={0}, use_global_device_ids=true | all-gather | bytes 614400 | tf_op jit(solution)/shard_map/all_gather | solution.py:40
  23.1 0.0 all-gather.14.cloned.1.call-update
  23.1 0.0 all-gather.18.cloned.1.call-start
  23.2 0.9 split.11
  24.1 5.0 %all_gather.58 = bf16[2,32,2560]{2,1,0:T(8,128)(2,1)} all-gather(bf16[1,32,2560]{2,1,0:T(8,128)(2,1)S(1)} %split.11), channel_id=1, replica_groups=mesh['rep'=4,'fsdp_0'=4,'fsdp_1'=4,'fsdp_2'=2] {'fsdp_2'}, dimensions={0}, use_global_device_ids=true | all-gather | bytes 491520 | tf_op jit(solution)/shard_map/all_gather | solution.py:40
  29.1 0.0 all-gather.18.cloned.1.call-update
  29.1 0.0 all-gather.16.cloned.1.call-start
  29.1 27.2 %all-gather.14.cloned.1.call-done = bf16[16,24,2560]{2,1,0:T(8,128)(2,1)} async-done(((bf16[4,24,2560]{2,1,0:T(8,128)(2,1)}), bf16[16,24,2560]{2,1,0:T(8,128)(2,1)}) %all-gather.14.cloned.1.call-update) | async-done | bytes 1966096 | tf_op jit(solution)/shard_map/all_gather | solution.py:40
  56.3 0.0 all-gather.16.cloned.1.call-update
  56.3 0.0 all-gather.12.cloned.1.call-start
  56.4 9.8 %all_gather.48 = bf16[4,24,2560]{2,1,0:T(8,128)(2,1)S(1)} all-gather(bf16[1,24,2560]{2,1,0:T(8,128)(2,1)S(1)} %get-tuple-element.43), channel_id=1, replica_groups=mesh['rep'=4,'fsdp_0'=4,'fsdp_1'=4,'fsdp_2'=2] {'fsdp_0'}, dimensions={0}, use_global_device_ids=true | all-gather | bytes 614400 | tf_op jit(solution)/shard_map/all_gather | solution.py:40
  66.2 9.3 %all-gather = bf16[8,24,2560]{2,1,0:T(8,128)(2,1)S(1)} all-gather(bf16[4,24,2560]{2,1,0:T(8,128)(2,1)S(1)} %all_gather.48), channel_id=2, replica_groups=mesh['rep'=4,'fsdp_0'=4,'fsdp_1'=4,'fsdp_2'=2] {'fsdp_2'}, dimensions={0}, use_global_device_ids=true | all-gather | bytes 1474560 | tf_op jit(solution)/shard_map/all_gather | solution.py:40
  75.6 1.0 copy.66
  76.6 0.0 all-gather.12.cloned.1.call-update
  76.6 0.0 all-gather.20.cloned.1.call-start
  76.7 5.3 %all-gather.18.cloned.1.call-done = bf16[8,32,2560]{2,1,0:T(8,128)(2,1)} async-done(((bf16[2,32,2560]{2,1,0:T(8,128)(2,1)}), bf16[8,32,2560]{2,1,0:T(8,128)(2,1)}) %all-gather.18.cloned.1.call-update) | async-done | bytes 1310736 | tf_op jit(solution)/shard_map/all_gather | solution.py:40
  82.0 0.0 reduce-scatter.2.cloned.1.call-start
  82.1 4.0 copy.60
  86.0 3.9 copy.61
  89.9 3.9 copy.64
  93.9 0.1 fusion.38
  94.1 10.9 %fusion.48 = (f32[20,384]{1,0:T(8,128)S(1)}, f32[20,384,384]{1,2,0:T(8,128)}) fusion(pred[384,384]{0,1:T(8,128)(4,1)S(1)} %fusion.38, bf16[384,20,128]{0,2,1:T(8,128)(2,1)} %bitcast.85, bf16[384,20,128]{0,2,1:T(8,128)(2,1)} %bitcast.83), kind=kOutput, calls=%fused_computation.46 | convolution fusion | flops 766771584 | bytes 15906816 | tf_op jit(solution)/shard_map/sub | solution.py:80
  105.0 6.4 %fusion.23 = bf16[20,384,128]{1,2,0:T(8,128)(2,1)S(1)} fusion(bf16[384,20,128]{0,2,1:T(8,128)(2,1)} %bitcast.76, f32[20,384,384]{1,2,0:T(8,128)} %get-tuple-element.46, f32[20,384]{1,0:T(8,128)S(1)} %get-tuple-element.45), kind=kOutput, calls=%fused_computation.26 | convolution fusion | flops 761856000 | bytes 15759360 | tf_op jit(solution)/shard_map/hqk,khd->qhd/dot_general | solution.py:83
  111.5 1.2 copy-done.8
  112.7 10.0 %convolution_convert_fusion = bf16[2560,2560]{1,0:T(8,128)(2,1)} fusion(bf16[384,2560]{0,1:T(8,128)(2,1)S(1)} %bitcast.93, bf16[1,384,2560]{2,1,0:T(8,128)(2,1)S(1)} %copy-done), kind=kOutput, calls=%fused_computation.2 | convolution fusion | flops 5039718400 | bytes 17039360 | tf_op jit(solution)/shard_map/dot_general | solution.py:147
  122.7 0.0 reduce-scatter.2.cloned.1.call-update
  123.4 20.2 %all-gather.16.cloned.1.call-done = bf16[8,4,24,2560]{3,2,1,0:T(8,128)(2,1)} async-done(((bf16[4,4,24,2560]{3,2,1,0:T(8,128)(2,1)}), bf16[8,4,24,2560]{3,2,1,0:T(8,128)(2,1)}) %all-gather.16.cloned.1.call-update) | async-done | bytes 3932176 | tf_op jit(solution)/shard_map/all_gather | solution.py:40
  143.5 4.5 copy.67
  148.0 80.3 %all-gather.12.cloned.1.call-done = bf16[8,4,24,2560]{3,2,0,1:T(8,128)(2,1)} async-done(((bf16[2,4,24,2560]{3,2,0,1:T(8,128)(2,1)}), bf16[8,4,24,2560]{3,2,0,1:T(8,128)(2,1)}) %all-gather.12.cloned.1.call-update) | async-done | bytes 3932176 | tf_op jit(solution)/shard_map/all_gather | solution.py:40
  228.3 68.7 %all-gather.20.cloned.1.call-done = bf16[16,2,32,2560]{3,2,1,0:T(8,128)(2,1)} async-done(((bf16[4,2,32,2560]{3,2,1,0:T(8,128)(2,1)}), bf16[16,2,32,2560]{3,2,1,0:T(8,128)(2,1)}) %all-gather.20.cloned.1.call-update) | async-done | bytes 5242896 | tf_op jit(solution)/shard_map/all_gather | solution.py:40
  297.0 9.4 %pad_maximum_fusion = bf16[32,80,2560]{2,1,0:T(8,128)(2,1)S(1)} fusion(bf16[32,32,2560]{2,1,0:T(8,128)(2,1)} %bitcast.78, bf16[32,24,2560]{2,1,0:T(8,128)(2,1)} %bitcast.73, bf16[32,24,2560]{2,1,0:T(8,128)(2,1)} %bitcast.79), kind=kLoop, calls=%fused_computation.3 | loop fusion | flops 39321600 | bytes 26214400 | tf_op jit(solution)/shard_map/concatenate | solution.py:62
  306.4 7.0 %convolution_convert_fusion.1 = bf16[2560,384]{1,0:T(8,128)(2,1)S(1)} fusion(bf16[2560,2560]{1,0:T(8,128)(2,1)S(1)} %bitcast.74, bf16[1,384,2560]{2,1,0:T(8,128)(2,1)S(1)} %copy-done), kind=kOutput, calls=%fused_computation.18 | convolution fusion | flops 5034147840 | bytes 17039360 | tf_op jit(solution)/shard_map/dot_general | solution.py:138
  313.5 3.2 fusion.26
  316.6 4.0 copy.75
  320.6 7.5 %fusion.49 = f32[20,384,384]{1,2,0:T(8,128)} fusion(bf16[384,20,128]{0,2,1:T(8,128)(2,1)} %bitcast.88, bf16[384,20,128]{0,2,1:T(8,128)(2,1)S(1)} %bitcast.77), kind=kOutput, calls=%fused_computation.47 | convolution fusion | flops 754974720 | bytes 15728640 | tf_op jit(solution)/shard_map/qhd,khd->hqk/dot_general | solution.py:96
  328.2 20.1 %fusion.32 = bf16[20,384,128]{1,2,0:T(8,128)(2,1)} fusion(bf16[384,20,128]{0,2,1:T(8,128)(2,1)} %bitcast.86, f32[20,384,384]{1,2,0:T(8,128)} %fusion.49, f32[20,384,384]{1,2,0:T(8,128)} %get-tuple-element.46, f32[20,384]{1,0:T(8,128)S(1)} %get-tuple-element.45), kind=kOutput, calls=%fused_computation.29 | convolution fusion | flops 776609664 | bytes 27555840 | tf_op jit(solution)/shard_map/hqk,qhd->khd/dot_general | solution.py:104
  348.3 4.0 copy.74
  352.3 19.5 %fusion.29 = bf16[20,384,128]{1,2,0:T(8,128)(2,1)} fusion(bf16[384,20,128]{0,2,1:T(8,128)(2,1)S(1)} %bitcast.84, f32[20,384,384]{1,2,0:T(8,128)} %fusion.49, f32[20,384,384]{1,2,0:T(8,128)} %get-tuple-element.46, f32[20,384]{1,0:T(8,128)S(1)} %get-tuple-element.45), kind=kOutput, calls=%fused_computation.28 | convolution fusion | flops 776609664 | bytes 27555840 | tf_op jit(solution)/shard_map/hqk,khd->qhd/dot_general | solution.py:101
  371.8 4.0 copy.73
  375.7 10.4 %fusion.16 = bf16[1,384,2560]{2,1,0:T(8,128)(2,1)} fusion(bf16[384,2560]{0,1:T(8,128)(2,1)} %bitcast.94, bf16[2560,2560]{1,0:T(8,128)(2,1)} %bitcast.75, bf16[1,384,2560]{2,1,0:T(8,128)(2,1)} %param.14), kind=kOutput, calls=%fused_computation.19 | convolution fusion | flops 5036113920 | bytes 19005440 | tf_op jit(solution)/shard_map/dot_general | solution.py:137
  386.1 54.8 %reduce-scatter.2.cloned.1.call-done = bf16[80,2560]{1,0:T(8,128)(2,1)} async-done(((bf16[2560,2560]{1,0:T(8,128)(2,1)}), bf16[80,2560]{1,0:T(8,128)(2,1)}) %reduce-scatter.2.cloned.1.call-update) | async-done | bytes 409616 | tf_op jit(solution)/shard_map/reduce_scatter | solution.py:146
  440.9 2.3 fusion.39
  443.2 3.4 conditional.4
  443.2 1.9 collective-permute-start
  445.1 1.5 collective-permute-done
  446.6 1.9 fusion.40
  (26 shorter events, 0.1 us)
Async XLA Ops:
  8.0 104.7 %copy-start = (bf16[1,384,2560]{2,1,0:T(8,128)(2,1)S(1)}, bf16[1,384,2560]{2,1,0:T(8,128)(2,1)}, u32[]{:S(2)}) copy-start(bf16[1,384,2560]{2,1,0:T(8,128)(2,1)} %param.15) | copy-start | bytes 5898244
  8.0 48.3 %all-gather.14.cloned.1.call-start = ((), (), s32[]{:S(2)}) async-start(), calls=%async_computation.3 | async-start | bytes 2457600 | tf_op jit(solution)/shard_map/all_gather | solution.py:40
  23.1 58.9 %all-gather.18.cloned.1.call-start = ((), (), s32[]{:S(2)}) async-start(), calls=%async_computation.5 | async-start | bytes 1638400 | tf_op jit(solution)/shard_map/all_gather | solution.py:40
  29.1 114.5 %all-gather.16.cloned.1.call-start = ((), (), s32[]{:S(2)}) async-start(), calls=%async_computation.4 | async-start | bytes 5898240 | tf_op jit(solution)/shard_map/all_gather | solution.py:40
  56.3 172.0 %all-gather.12.cloned.1.call-start = ((), (), s32[]{:S(2)}) async-start(), calls=%async_computation.2 | async-start | bytes 4915200 | tf_op jit(solution)/shard_map/all_gather | solution.py:40
  76.6 220.4 %all-gather.20.cloned.1.call-start = ((), (), s32[]{:S(2)}) async-start(), calls=%async_computation.6 | async-start | bytes 6553600 | tf_op jit(solution)/shard_map/all_gather | solution.py:40
  82.0 11.9 %copy-start.7 = (s32[1,384]{1,0:T(1,128)S(1)}, s32[1,384]{1,0:T(1,128)}, u32[]{:S(2)}) copy-start(s32[1,384]{1,0:T(1,128)} %param.16) | copy-start | bytes 4612
  82.0 358.9 %reduce-scatter.2.cloned.1.call-start = ((), (), s32[]{:S(2)}) async-start(), calls=%async_computation.1 | async-start | bytes 13516800 | tf_op jit(solution)/shard_map/reduce_scatter | solution.py:146
  111.5 1.2 copy-start.8
  297.0 16.4 %slice-start = ((s8[11796480]{0:T(1024)(128)(4,1)}), s8[4194304]{0:T(1024)(128)(4,1)S(1)}, s32[]{:S(2)}) async-start(s8[11796480]{0:T(1024)(128)(4,1)} %bitcast.95), calls=%async_computation.7 | async-start | bytes 8388608
  297.0 16.4 %slice-start.1 = ((s8[11796480]{0:T(1024)(128)(4,1)}), s8[4194304]{0:T(1024)(128)(4,1)S(1)}, s32[]{:S(2)}) async-start(s8[11796480]{0:T(1024)(128)(4,1)} %bitcast.95), calls=%async_computation.8 | async-start | bytes 8388608
  306.4 7.0 %copy-start.2 = (bf16[32,80,2560]{2,1,0:T(8,128)(2,1)}, bf16[32,80,2560]{2,1,0:T(8,128)(2,1)S(1)}, u32[]{:S(2)}) copy-start(bf16[32,80,2560]{2,1,0:T(8,128)(2,1)S(1)} %pad_maximum_fusion) | copy-start | bytes 39321604
  306.4 7.1 %slice-start.2 = ((s8[11796480]{0:T(1024)(128)(4,1)}), s8[3407872]{0:T(1024)(128)(4,1)S(1)}, s32[]{:S(2)}) async-start(s8[11796480]{0:T(1024)(128)(4,1)} %bitcast.95), calls=%async_computation.9 | async-start | bytes 6815744
  313.4 3.3 copy-start.5
  313.4 7.2 %copy-start.3 = (bf16[1,384,2560]{1,2,0:T(8,128)(2,1)S(1)}, bf16[1,384,2560]{1,2,0:T(8,128)(2,1)}, u32[]{:S(2)}) copy-start(bf16[1,384,2560]{1,2,0:T(8,128)(2,1)} %copy.64) | copy-start | bytes 5898244
  328.2 24.1 %copy-start.4 = (bf16[1,384,2560]{1,2,0:T(8,128)(2,1)S(1)}, bf16[1,384,2560]{1,2,0:T(8,128)(2,1)}, u32[]{:S(2)}) copy-start(bf16[1,384,2560]{1,2,0:T(8,128)(2,1)} %copy.61) | copy-start | bytes 5898244
  375.7 65.2 %copy-start.6 = (bf16[1,80,2560]{2,1,0:T(8,128)(2,1)S(1)}, bf16[1,80,2560]{2,1,0:T(8,128)(2,1)}, u32[]{:S(2)}) copy-start(bf16[1,80,2560]{2,1,0:T(8,128)(2,1)} %param.17) | copy-start | bytes 1228804
  375.7 72.7 %copy-start.1 = (bf16[1,384,2560]{2,1,0:T(8,128)(2,1)S(1)}, bf16[1,384,2560]{2,1,0:T(8,128)(2,1)}, u32[]{:S(2)}) copy-start(bf16[1,384,2560]{2,1,0:T(8,128)(2,1)} %param.15) | copy-start | bytes 5898244
  443.2 3.4 collective-permute-start
Sparse Core Ops, SparseCore 0:
  23.2 33.0 all-gather.13
  58.0 23.9 all-gather.17
  83.6 59.8 all-gather.15
  145.6 82.6 all-gather.11
  229.8 67.1 all-gather.19
Sparse Core Ops, SparseCore 1:
  122.8 318.0 reduce-scatter.1
where the time goes:
time: 456 us
  waiting for transfers between devices  258 us (57%)
  matrix products  95.1 us (21%)
  blocking collectives  38 us (8%)
  local copies, waits for them, and re-layouts  32.6 us (7%)
  between operations  16 us (4%)
  other arithmetic  13.7 us (3%)
    all_gather x5, waiting for transfers between devices, stacked_from(): tiles = lax.all_gather(tiles, axes[k])  202 us
    reduce_scatter x1, waiting for transfers between devices, on_device(): lax.psum_scatter(lax.dot_general(context, grad_local, (((0,), (0,)), ((),...  54.8 us
    all_gather x4, blocking collectives, stacked_from(): tiles = lax.all_gather(tiles, axes[k])  38 us
    unnamed x30, local copies, waits for them, and re-layouts  25.1 us
    dot_general x1, matrix products, attend_local_back(): jnp.einsum('hqk,qhd->khd', score_grad, query_heads, preferred_element_typ...  20.1 us
    dot_general x1, matrix products, attend_local_back(): jnp.einsum('hqk,khd->qhd', score_grad, key_heads, preferred_element_type=...  19.5 us
    sub x1, matrix products, attend_local(): exponents = jnp.exp(scores - row_peaks)  10.9 us
    dot_general x1, matrix products, on_device(): projected = jnp.dot(context, gathered, preferred_element_type=jnp.float32)  10.4 us
  transfers between devices with their start and end apart: 7, of which 7 were waited for; matrix products, arithmetic and copies ran while one was open for 30% of the time, Pallas kernels for 0%

commit v1 on v0

v1 whole, which is shorter than its diff:
```python
import functools

import jax
import jax.numpy as jnp
from jax import lax
from jax.experimental import pallas as pl
from jax.experimental.pallas import tpu as pltpu
from jax.sharding import Mesh
from jax.sharding import PartitionSpec as P

HEADS = 20
HEAD_SIZE = 128
TOK = 384
WIDTH = 2560
SHARD = 80
AX, AZ, AY = "fsdp_0", "fsdp_1", "fsdp_2"
FSDP = (AX, AZ, AY)

momentum_decay = 0.9
learning_rate = 0.0003
score_scale = HEAD_SIZE ** (-0.5)

FORWARD_HEADS = 5
BACKWARD_HEADS = 2

bf16 = jnp.bfloat16
f32 = jnp.float32


def swapped(block, axis, distance):
    count = lax.axis_size(axis)
    return lax.ppermute(block, axis, [(i, i ^ (1 << distance)) for i in range(count)])


def dot(a, b, dims):
    return lax.dot_general(a, b, (dims, ((), ())), preferred_element_type=f32)


def mask_bias(doc_col, doc_row):
    rows = lax.broadcasted_iota(jnp.int32, (TOK, TOK), 0)
    cols = lax.broadcasted_iota(jnp.int32, (TOK, TOK), 1)
    allowed = (cols <= rows) & (doc_col == doc_row)
    return jnp.where(allowed, 0.0, -1e30).astype(f32)


def softmax_rows(q, k, bias):
    scores = dot(q, k, ((1,), (1,))) * score_scale + bias
    peak = jnp.max(scores, axis=-1, keepdims=True)
    e = jnp.exp(scores - peak)
    return e * (1.0 / jnp.sum(e, axis=-1, keepdims=True))


def forward_kernel(q, k, v, og, doc_col, doc_row, *refs):
    context, term, bias = refs[-3:]

    @pl.when(pl.program_id(0) == 0)
    def _():
        bias[...] = mask_bias(doc_col[:, :1], doc_row[:1, :])

    for h in range(FORWARD_HEADS):
        cols = slice(h * HEAD_SIZE, (h + 1) * HEAD_SIZE)
        probs = softmax_rows(q[:, cols], k[:, cols], bias[...])
        context[:, cols] = dot(probs.astype(bf16), v[:, cols], ((1,), (0,))).astype(bf16)
    term[...] = dot(context[...], og[...], ((0,), (0,))).astype(bf16)


def whole(shape):
    return pl.BlockSpec(shape, lambda i: (0, 0), pipeline_mode=pl.Buffered(1))


def forward_pass(q, k, v, og, doc_col, doc_row, first, count, earlier=()):
    size = FORWARD_HEADS * HEAD_SIZE
    column = pl.BlockSpec((TOK, size), lambda i: (0, i + first))
    return pl.pallas_call(
        forward_kernel,
        out_shape=[jax.ShapeDtypeStruct((TOK, WIDTH), bf16), jax.ShapeDtypeStruct((WIDTH, WIDTH), bf16)],
        grid_spec=pltpu.PrefetchScalarGridSpec(
            num_scalar_prefetch=0,
            grid=(count,),
            in_specs=[column, column, column, whole((TOK, WIDTH)), whole((TOK, HEAD_SIZE)), whole((8, TOK))]
            + [pl.BlockSpec(memory_space=pl.ANY)] * len(earlier),
            out_specs=[column, pl.BlockSpec((size, WIDTH), lambda i: (i + first, 0))],
            scratch_shapes=[pltpu.VMEM((TOK, TOK), f32)],
        ),
        input_output_aliases={6 + i: i for i in range(len(earlier))},
        compiler_params=pltpu.CompilerParams(
            dimension_semantics=("arbitrary",), vmem_limit_bytes=60 * 1024 * 1024
        ),
        cost_estimate=pl.CostEstimate(
            flops=int(1.65e9) * count, transcendentals=750000 * count, bytes_accessed=int(6e6) * count
        ),
        name="attend_forward",
    )(q, k, v, og, doc_col, doc_row, *earlier)


def backward_kernel(q, k, v, og, ctx, res, doc_col, doc_row, w_rows, w_cols, block_out, qg, kg, vg, bias):
    @pl.when(pl.program_id(0) == 0)
    def _():
        bias[...] = mask_bias(doc_col[:, :1], doc_row[:1, :])

    cg_all = dot(og[...], w_rows[...], ((1,), (1,))).astype(bf16)
    block_out[...] = (res[...].astype(f32) + dot(ctx[...], w_cols[...], ((1,), (0,)))).astype(bf16)
    for h in range(BACKWARD_HEADS):
        cols = slice(h * HEAD_SIZE, (h + 1) * HEAD_SIZE)
        qh, kh, vh, cg = q[:, cols], k[:, cols], v[:, cols], cg_all[:, cols]
        probs = softmax_rows(qh, kh, bias[...])
        vg[:, cols] = dot(probs.astype(bf16), cg, ((0,), (0,))).astype(bf16)
        pg = dot(cg, vh, ((1,), (1,)))
        delta = jnp.sum(pg * probs, axis=-1, keepdims=True)
        ds = (probs * (pg - delta) * score_scale).astype(bf16)
        qg[:, cols] = dot(ds, kh, ((1,), (0,))).astype(bf16)
        kg[:, cols] = dot(ds, qh, ((0,), (0,))).astype(bf16)


def backward_pass(q, k, v, og, ctx, res, doc_col, doc_row, weight):
    size = BACKWARD_HEADS * HEAD_SIZE
    column = pl.BlockSpec((TOK, size), lambda i: (0, i))
    return pl.pallas_call(
        backward_kernel,
        out_shape=[jax.ShapeDtypeStruct((TOK, WIDTH), bf16)] * 4,
        grid_spec=pltpu.PrefetchScalarGridSpec(
            num_scalar_prefetch=0,
            grid=(HEADS // BACKWARD_HEADS,),
            in_specs=[column, column, column, whole((TOK, WIDTH)), whole((TOK, WIDTH)), column]
            + [whole((TOK, HEAD_SIZE)), whole((8, TOK))]
            + [pl.BlockSpec((size, WIDTH), lambda i: (i, 0)), pl.BlockSpec((WIDTH, size), lambda i: (0, i))],
            out_specs=[column] * 4,
            scratch_shapes=[pltpu.VMEM((TOK, TOK), f32)],
        ),
        compiler_params=pltpu.CompilerParams(
            dimension_semantics=("arbitrary",), vmem_limit_bytes=60 * 1024 * 1024
        ),
        cost_estimate=pl.CostEstimate(flops=int(14e9), transcendentals=int(3e6), bytes_accessed=int(46e6)),
        name="attend_backward",
    )(q, k, v, og, ctx, res, doc_col, doc_row, weight, weight)


def on_device(query_rows, key_rows, value_rows, residual_in, out_grad, doc_ids, out_weight, momentum, step_index):
    q, k, v = query_rows[0], key_rows[0], value_rows[0]
    og = out_grad[0]
    shard = out_weight[0]
    y = lax.axis_index(AY)
    other = swapped(shard, AY, 0)
    both = jnp.concatenate([jnp.where(y == 0, shard, other), jnp.where(y == 0, other, shard)], axis=0)
    doc_col = jnp.broadcast_to(doc_ids[0][:, None], (TOK, HEAD_SIZE))
    doc_row = jnp.broadcast_to(doc_ids, (8, TOK))
    some = forward_pass(q, k, v, og, doc_col, doc_row, 0, 2)
    *some, both = lax.optimization_barrier((*some, both))
    weight = lax.all_gather(both, (AX, AZ), tiled=True)
    context, term = forward_pass(q, k, v, og, doc_col, doc_row, 2, 2, some)
    pair = lax.psum_scatter(term, (AX, AZ), scatter_dimension=0, tiled=True)
    block_out, query_grad, key_grad, value_grad = backward_pass(
        q, k, v, og, context, residual_in[0], doc_col, doc_row, weight
    )
    pair, query_grad = lax.optimization_barrier((pair, query_grad))
    sent = jnp.where(y == 0, pair[SHARD:], pair[:SHARD])
    kept = jnp.where(y == 0, pair[:SHARD], pair[SHARD:])
    weight_grad = kept.astype(f32) + swapped(sent, AY, 0).astype(f32)
    new_momentum = momentum_decay * momentum[0] + weight_grad
    stepped = (shard.astype(f32) - learning_rate * new_momentum).astype(bf16)
    levels = lax.axis_size("rep").bit_length() - 1
    branches = [functools.partial(swapped, axis="rep", distance=level) for level in range(levels)]
    partner = lax.switch(step_index[0] % levels, branches, stepped)
    new_weight = ((stepped.astype(f32) + partner.astype(f32)) * 0.5).astype(bf16)
    return (
        block_out[None],
        query_grad[None],
        key_grad[None],
        value_grad[None],
        new_weight[None],
        new_momentum[None],
    )


def solution(mesh):
    torus = Mesh(mesh.devices.reshape(mesh.shape["rep"], 4, 4, 2), ("rep", AX, AZ, AY))
    rows = P("rep", FSDP, None)
    return jax.shard_map(
        on_device,
        mesh=torus,
        in_specs=(rows, rows, rows, rows, rows, P("rep", FSDP), rows, rows, P()),
        out_specs=(rows,) * 6,
        check_vma=False,
    )
```

time: 456 us -> 245 us (0.54)
  waiting for transfers between devices: 258 us -> 156 us
  matrix products: 95.1 us -> 0 us
  Pallas kernels: 0 us -> 60.9 us
  blocking collectives: 38 us -> 0 us
  local copies, waits for them, and re-layouts: 32.6 us -> 1.4 us
  other arithmetic: 13.7 us -> 7.04 us
    all_gather x5 -> x1, waiting for transfers between devices: 202 us -> 82.7 us  [on_device(): weight = lax.all_gather(both, (AX, AZ), tiled=True)]
    dot_general x8 -> x0, matrix products: 84.1 us -> none  [the longest x1 20.1 us: attend_local_back(): jnp.einsum('hqk,qhd->khd', score_grad, query_heads, preferred_element_typ...]
    pallas_call x0 -> x3, Pallas kernels: none -> 60.9 us  [the longest x1 36 us: backward_pass(): pl.pallas_call(backward_kernel, out_shape=[jax.ShapeDtypeStruct((TOK, WID...]
    all_gather x4 -> x0, blocking collectives: 38 us -> none  [stacked_from(): tiles = lax.all_gather(tiles, axes[k])]
    unnamed x30 -> x4, local copies, waits for them, and re-layouts: 25.1 us -> 0.01 us
    sub x1 -> x0, matrix products: 10.9 us -> none  [attend_local(): exponents = jnp.exp(scores - row_peaks)]
    concatenate x1, other arithmetic: 9.37 us -> 0.94 us  [on_device(): jnp.concatenate([jnp.where(y == 0, shard, other), jnp.where(y == 0, other...]
    reduce_scatter x1, waiting for transfers between devices: 54.8 us -> 63.1 us  [on_device(): pair = lax.psum_scatter(term, (AX, AZ), scatter_dimension=0, tiled=True)]
  transfers between devices with their start and end apart: 7 -> 5, of which waited for: 7 -> 4; matrix products, arithmetic and copies ran while one was open for 30% -> 1% of each run, Pallas kernels for 0% -> 25%
where the time goes in v1:
time: 245 us
  waiting for transfers between devices  156 us (64%)
  Pallas kernels  60.9 us (25%)
  between operations  14.7 us (6%)
  other arithmetic  7.04 us (3%)
  starting transfers between devices  5.31 us (2%)
    all_gather x1, waiting for transfers between devices, on_device(): weight = lax.all_gather(both, (AX, AZ), tiled=True)  82.7 us
    reduce_scatter x1, waiting for transfers between devices, on_device(): pair = lax.psum_scatter(term, (AX, AZ), scatter_dimension=0, tiled=True)  63.1 us
    pallas_call x1, Pallas kernels, backward_pass(): pl.pallas_call(backward_kernel, out_shape=[jax.ShapeDtypeStruct((TOK, WID...  36 us
    pallas_call x2, Pallas kernels, forward_pass(): pl.pallas_call(forward_kernel, out_shape=[jax.ShapeDtypeStruct((TOK, WIDT...  24.9 us
    ppermute x3, waiting for transfers between devices, swapped(): lax.ppermute(block, axis, [(i, i ^ 1 << distance) for i in range(count)])  9.78 us
    ppermute x3, starting transfers between devices, swapped(): lax.ppermute(block, axis, [(i, i ^ 1 << distance) for i in range(count)])  5.23 us
  transfers between devices with their start and end apart: 5, of which 4 were waited for; matrix products, arithmetic and copies ran while one was open for 1% of the time, Pallas kernels for 25%

profile of v1, /device:TPU:1, one launch (start us, length us, event | category | flops | bytes accessed | tf_op | source)
XLA Modules:
  0.0 245.0 jit_solution(5730409556032652870)
XLA Ops:
  7.2 0.0 all-gather.2.cloned.1.call-start
  7.2 2.2 collective-permute-start.2
  9.4 0.7 reduce
  10.1 0.6 broadcast_in_dim.32.doc_row
  10.7 0.8 broadcast_in_dim.31.doc_col
  11.5 0.0 copy-start
  11.5 12.4 %attend_forward.2 = (bf16[384,2560]{1,0:T(8,128)(2,1)}, bf16[2560,2560]{1,0:T(8,128)(2,1)}) custom-call(bf16[384,2560]{1,0:T(8,128)(2,1)} %bitcast.27, bf16[384,2560]{1,0:T(8,128)(2,1)} %bitcast.30, bf16[384,2560]{1,0:T(8,128)(2,1)} %bitcast.33, bf16[384,2560]{1,0:T(8,128)(2,1)} %bitcast.36, s32[384,128]{1,0:T(8,128)} %broadcast_in_dim.31.doc_col, ...), custom_call_target="tpu_custom_call" | custom-call | flops 3300000000 | bytes 12000000 | tf_op jit(solution)/shard_map/attend_forward/pallas_call | solution.py:74
  23.9 0.0 collective-permute-done.2
  23.9 0.0 copy-done
  23.9 0.1 broadcast_select_fusion.2
  24.0 0.9 pad_maximum_fusion
  24.9 0.0 all-gather.2.cloned.1.call-update
  25.0 0.0 reduce-scatter.2.cloned.1.call-start
  25.0 12.5 %attend_forward.3 = (bf16[384,2560]{1,0:T(8,128)(2,1)}, bf16[2560,2560]{1,0:T(8,128)(2,1)}) custom-call(bf16[384,2560]{1,0:T(8,128)(2,1)} %bitcast.28, bf16[384,2560]{1,0:T(8,128)(2,1)} %bitcast.31, bf16[384,2560]{1,0:T(8,128)(2,1)} %bitcast.34, bf16[384,2560]{1,0:T(8,128)(2,1)} %bitcast.37, ...), custom_call_target="tpu_custom_call", output_to_operand_aliasing={{0}: (6, {}), {1}: (7, {})} | custom-call | flops 3300000000 | bytes 12000000 | tf_op jit(solution)/shard_map/attend_forward/pallas_call | solution.py:74
  37.5 0.0 reduce-scatter.2.cloned.1.call-update
  37.5 82.7 %all-gather.2.cloned.1.call-done.w_rows.w_cols = bf16[2560,2560]{1,0:T(8,128)(2,1)} async-done(((bf16[160,2560]{1,0:T(8,128)(2,1)}), bf16[2560,2560]{1,0:T(8,128)(2,1)}) %all-gather.2.cloned.1.call-update) | async-done | bytes 13107216 | tf_op jit(solution)/shard_map/all_gather | solution.py:149
  120.2 0.0 copy-start.1
  120.2 36.0 %attend_backward.1 = (bf16[384,2560]{1,0:T(8,128)(2,1)}, bf16[384,2560]{1,0:T(8,128)(2,1)}, bf16[384,2560]{1,0:T(8,128)(2,1)}, bf16[384,2560]{1,0:T(8,128)(2,1)}) custom-call(bf16[384,2560]{1,0:T(8,128)(2,1)} %bitcast.29, bf16[384,2560]{1,0:T(8,128)(2,1)} %bitcast.32, bf16[384,2560]{1,0:T(8,128)(2,1)} %bitcast.35, bf16[384,2560]{1,0:T(8,128)(2,1)} %bitcast.38, ...), custom_call_target="tpu_custom_call" | custom-call | flops 14000000000 | bytes 46000000 | tf_op jit(solution)/shard_map/attend_backward/pallas_call | solution.py:118
  156.3 63.1 %reduce-scatter.2.cloned.1.call-done = bf16[160,2560]{1,0:T(8,128)(2,1)} async-done(((bf16[2560,2560]{1,0:T(8,128)(2,1)}), bf16[160,2560]{1,0:T(8,128)(2,1)}) %reduce-scatter.2.cloned.1.call-update) | async-done | bytes 819216 | tf_op jit(solution)/shard_map/reduce_scatter | solution.py:151
  219.4 1.2 broadcast_select_fusion
  220.6 1.3 collective-permute-start.3
  222.5 8.3 %collective-permute-done.3 = bf16[80,2560]{1,0:T(8,128)(2,1)S(1)} collective-permute-done((bf16[80,2560]{1,0:T(8,128)(2,1)S(1)}, bf16[80,2560]{1,0:T(8,128)(2,1)S(1)}, u32[]{:S(2)}, u32[]{:S(2)}) %collective-permute-start.3) | collective-permute-done | bytes 409632 | tf_op jit(solution)/shard_map/ppermute | solution.py:32
  230.8 0.0 copy-done.1
  230.8 2.3 fusion.1
  233.1 3.2 %conditional.4 = (bf16[80,2560]{1,0:T(8,128)(2,1)}) conditional(s32[]{:T(128)} %clamp.3, bf16[80,2560]{1,0:T(8,128)(2,1)S(1)} %get-tuple-element.44, bf16[80,2560]{1,0:T(8,128)(2,1)S(1)} %get-tuple-element.44), branch_computations={%region_1.2_spmd, %region_2.3_spmd} | conditional | bytes 1638448
  233.1 1.7 collective-permute-start
  234.8 1.5 collective-permute-done
  236.3 1.9 fusion
Async XLA Ops:
  7.2 113.0 %all-gather.2.cloned.1.call-start = ((), (), s32[]{:S(2)}) async-start(), calls=%async_computation.1 | async-start | bytes 13926400 | tf_op jit(solution)/shard_map/all_gather | solution.py:149
  7.2 16.7 %collective-permute-start.2 = (bf16[80,2560]{1,0:T(8,128)(2,1)}, bf16[80,2560]{1,0:T(8,128)(2,1)S(1)}, u32[]{:S(2)}, u32[]{:S(2)}) collective-permute-start(bf16[80,2560]{1,0:T(8,128)(2,1)} %bitcast.39), channel_id=1, source_target_pairs={{0,1},{1,0},{2,3},{3,2},{4,5},{5,4},{6,7},{7,6},{8,9},{9,8},{10,11... | collective-permute-start | bytes 1228808 | tf_op jit(solution)/shard_map/ppermute | solution.py:32
  11.5 12.4 %copy-start = (bf16[1,80,2560]{2,1,0:T(8,128)(2,1)S(1)}, bf16[1,80,2560]{2,1,0:T(8,128)(2,1)}, u32[]{:S(2)}) copy-start(bf16[1,80,2560]{2,1,0:T(8,128)(2,1)} %param.17) | copy-start | bytes 1228804
  25.0 194.4 %reduce-scatter.2.cloned.1.call-start = ((), (), s32[]{:S(2)}) async-start(), calls=%async_computation.2 | async-start | bytes 13926400 | tf_op jit(solution)/shard_map/reduce_scatter | solution.py:151
  120.2 110.6 %copy-start.1 = (f32[1,80,2560]{2,1,0:T(8,128)S(1)}, f32[1,80,2560]{2,1,0:T(8,128)}, u32[]{:S(2)}) copy-start(f32[1,80,2560]{2,1,0:T(8,128)} %param.18) | copy-start | bytes 2457604
  220.6 10.2 %collective-permute-start.3 = (bf16[80,2560]{1,0:T(8,128)(2,1)S(1)}, bf16[80,2560]{1,0:T(8,128)(2,1)S(1)}, u32[]{:S(2)}, u32[]{:S(2)}) collective-permute-start(bf16[80,2560]{1,0:T(8,128)(2,1)S(1)} %broadcast_select_fusion), channel_id=1, source_target_pairs={{0,1},{1,0},{2,3},{3,2},{4,5},{5,4},{6,7},{7,6},{8,9},{9,8},{10,11... | collective-permute-start | bytes 1228808 | tf_op jit(solution)/shard_map/ppermute | solution.py:32
  233.1 3.2 %collective-permute-start = (bf16[80,2560]{1,0:T(8,128)(2,1)S(1)}, bf16[80,2560]{1,0:T(8,128)(2,1)}, u32[]{:S(2)}, u32[]{:S(2)}) collective-permute-start(bf16[80,2560]{1,0:T(8,128)(2,1)S(1)} %param), channel_id=1, source_target_pairs={{0,32},{32,0},{64,96},{96,64},{1,33},{33,1},{65,97},{97,65},{2,34}... | collective-permute-start | bytes 1228808 | tf_op jit(solution)/shard_map/cond/branch_0_fun/ppermute | solution.py:32
Sparse Core Ops, SparseCore 0:
  25.1 95.0 all-gather.1
  123.7 95.6 reduce-scatter.1

commit v2 on v1

--- a/solution.py
+++ b/solution.py
@@ -32,6 +32,66 @@
     return lax.ppermute(block, axis, [(i, i ^ (1 << distance)) for i in range(count)])
 
 
+ROWS_A, ROWS_B, ROWS_C = 32, 16, 32
+OFF_A, OFF_B, OFF_C = 0, 32, 48
+
+def from_(block, axis, distance):
+    count = lax.axis_size(axis)
+    return lax.ppermute(block, axis, [(i, (i - distance) % count) for i in range(count)])
+
+
+def ring_gather(block, axis):
+    half = block.shape[0] // 2
+    up = from_(block, axis, 1)
+    down = from_(block, axis, -1)
+    two_low = from_(up[:half], axis, 1)
+    two_high = from_(down[half:], axis, -1)
+    return up, down, two_low, two_high
+
+
+def direct_gather(block, axis):
+    return jnp.concatenate(
+        [block, from_(block, axis, 1), from_(block, axis, 2), from_(block, axis, -1)], axis=0
+    )
+
+
+def gather_first(shard):
+    a = shard[OFF_A : OFF_A + ROWS_A][None]
+    b = shard[OFF_B : OFF_B + ROWS_B][None]
+    c = shard[OFF_C : OFF_C + ROWS_C][None]
+    b2 = jnp.concatenate([b, from_(b, AY, 1)], axis=0)
+    c2 = jnp.concatenate([c, from_(c, AY, 1)], axis=0)
+    return direct_gather(a, AX), b2, c2
+
+
+def gather_second(a4, b2, c2):
+    return direct_gather(b2, AX), direct_gather(c2, AZ), from_(a4, AY, 1)
+
+
+def gather_last(a4, b8, c8, a4_y):
+    parts = []
+    order = [(dx, dy) for dx in range(4) for dy in range(2)]
+    a_up, a_down, a_low, a_high = ring_gather(a4, AZ)
+    up, down, low, high = ring_gather(b8, AZ)
+    for array, dz, places in ((b8, 0, order), (up, 1, order), (down, 3, order), (low, 2, order[:4]), (high, 2, order[4:])):
+        parts.append((array, OFF_B, [(dx, dz, dy) for dx, dy in places]))
+    up, down, low, high = ring_gather(c8, AX)
+    for array, dx, places in ((c8, 0, order), (up, 1, order), (down, 3, order), (low, 2, order[:4]), (high, 2, order[4:])):
+        parts.append((array, OFF_C, [(dx, dz, dy) for dz, dy in places]))
+    mine = [
+        (a4, a4_y, [(k, 0) for k in range(4)]),
+        (a_up, None, [(k, 1) for k in range(4)]),
+        (a_down, None, [(k, 3) for k in range(4)]),
+        (a_low, None, [(k, 2) for k in range(2)]),
+        (a_high, None, [(k, 2) for k in range(2, 4)]),
+    ]
+    for array, across, places in mine:
+        across = from_(array, AY, 1) if across is None else across
+        parts.append((array, OFF_A, [(dx, dz, 0) for dx, dz in places]))
+        parts.append((across, OFF_A, [(dx, dz, 1) for dx, dz in places]))
+    return parts
+
+
 def dot(a, b, dims):
     return lax.dot_general(a, b, (dims, ((), ())), preferred_element_type=f32)
 
@@ -65,7 +125,7 @@
 
 
 def whole(shape):
-    return pl.BlockSpec(shape, lambda i: (0, 0), pipeline_mode=pl.Buffered(1))
+    return pl.BlockSpec(shape, lambda i, *_: (0, 0), pipeline_mode=pl.Buffered(1))
 
 
 def forward_pass(q, k, v, og, doc_col, doc_row, first, count, earlier=()):
@@ -93,16 +153,39 @@
     )(q, k, v, og, doc_col, doc_row, *earlier)
 
 
-def backward_kernel(q, k, v, og, ctx, res, doc_col, doc_row, w_rows, w_cols, block_out, qg, kg, vg, bias):
-    @pl.when(pl.program_id(0) == 0)
+PAIR = 2 * HEAD_SIZE
+
+
+def backward_kernel(places, pos, q, k, v, og, ctx, res, doc_col, doc_row, *refs):
+    parts = refs[: len(places)]
+    block_out, qg, kg, vg, bias, weight, sems = refs[len(places) :]
+    step = pl.program_id(0)
+
+    @pl.when(step == 0)
     def _():
+        copies = []
+        for part, (off, offsets) in zip(parts, places):
+            rows = part.shape[1]
+            for slot, (dx, dz, dy) in enumerate(offsets):
+                x = (pos[0] + dx) % 4
+                z = (pos[1] + dz) % 4
+                y = (pos[2] + dy) % 2
+                row = pl.multiple_of((x * 8 + z * 2 + y) * SHARD + off, 16)
+                copies.append(
+                    pltpu.make_async_copy(part.at[slot], weight.at[pl.ds(row, rows), :], sems.at[len(copies)])
+                )
+        for copy in copies:
+            copy.start()
         bias[...] = mask_bias(doc_col[:, :1], doc_row[:1, :])
-
-    cg_all = dot(og[...], w_rows[...], ((1,), (1,))).astype(bf16)
-    block_out[...] = (res[...].astype(f32) + dot(ctx[...], w_cols[...], ((1,), (0,)))).astype(bf16)
-    for h in range(BACKWARD_HEADS):
+        for copy in copies:
+            copy.wait()
+
+    rows = pl.ds(pl.multiple_of(step * PAIR, PAIR), PAIR)
+    cg_pair = dot(og[...], weight[rows, :], ((1,), (1,))).astype(bf16)
+    block_out[...] = (res[...].astype(f32) + dot(ctx[...], weight[:, rows], ((1,), (0,)))).astype(bf16)
+    for h in range(2):
         cols = slice(h * HEAD_SIZE, (h + 1) * HEAD_SIZE)
-        qh, kh, vh, cg = q[:, cols], k[:, cols], v[:, cols], cg_all[:, cols]
+        qh, kh, vh, cg = q[:, cols], k[:, cols], v[:, cols], cg_pair[:, cols]
         probs = softmax_rows(qh, kh, bias[...])
         vg[:, cols] = dot(probs.astype(bf16), cg, ((0,), (0,))).astype(bf16)
         pg = dot(cg, vh, ((1,), (1,)))
@@ -112,27 +195,32 @@
         kg[:, cols] = dot(ds, qh, ((0,), (0,))).astype(bf16)
 
 
-def backward_pass(q, k, v, og, ctx, res, doc_col, doc_row, weight):
-    size = BACKWARD_HEADS * HEAD_SIZE
-    column = pl.BlockSpec((TOK, size), lambda i: (0, i))
+def backward_pass(pos, q, k, v, og, ctx, res, doc_col, doc_row, parts):
+    places = [(off, offsets) for _, off, offsets in parts]
+    arrays = [array for array, _, _ in parts]
+    count = sum(len(offsets) for _, offsets in places)
+    column = pl.BlockSpec((TOK, PAIR), lambda i, *_: (0, i))
     return pl.pallas_call(
-        backward_kernel,
+        functools.partial(backward_kernel, places),
         out_shape=[jax.ShapeDtypeStruct((TOK, WIDTH), bf16)] * 4,
         grid_spec=pltpu.PrefetchScalarGridSpec(
-            num_scalar_prefetch=0,
-            grid=(HEADS // BACKWARD_HEADS,),
-            in_specs=[column, column, column, whole((TOK, WIDTH)), whole((TOK, WIDTH)), column]
-            + [whole((TOK, HEAD_SIZE)), whole((8, TOK))]
-            + [pl.BlockSpec((size, WIDTH), lambda i: (i, 0)), pl.BlockSpec((WIDTH, size), lambda i: (0, i))],
+            num_scalar_prefetch=1,
+            grid=(HEADS // 2,),
+            in_specs=[column, column, column, whole((TOK, WIDTH)), whole((TOK, WIDTH)), column, whole((TOK, HEAD_SIZE)), whole((8, TOK))]
+            + [pl.BlockSpec(memory_space=pl.ANY)] * len(arrays),
             out_specs=[column] * 4,
-            scratch_shapes=[pltpu.VMEM((TOK, TOK), f32)],
+            scratch_shapes=[
+                pltpu.VMEM((TOK, TOK), f32),
+                pltpu.VMEM((WIDTH, WIDTH), bf16),
+                pltpu.SemaphoreType.DMA((count,)),
+            ],
         ),
         compiler_params=pltpu.CompilerParams(
             dimension_semantics=("arbitrary",), vmem_limit_bytes=60 * 1024 * 1024
         ),
-        cost_estimate=pl.CostEstimate(flops=int(14e9), transcendentals=int(3e6), bytes_accessed=int(46e6)),
+        cost_estimate=pl.CostEstimate(flops=int(14e9), transcendentals=int(3e6), bytes_accessed=int(35e6)),
         name="attend_backward",
-    )(q, k, v, og, ctx, res, doc_col, doc_row, weight, weight)
+    )(pos, q, k, v, og, ctx, res, doc_col, doc_row, *arrays)
 
 
 def on_device(query_rows, key_rows, value_rows, residual_in, out_grad, doc_ids, out_weight, momentum, step_index):
@@ -140,17 +228,20 @@
     og = out_grad[0]
     shard = out_weight[0]
     y = lax.axis_index(AY)
-    other = swapped(shard, AY, 0)
-    both = jnp.concatenate([jnp.where(y == 0, shard, other), jnp.where(y == 0, other, shard)], axis=0)
+    pos = jnp.stack([lax.axis_index(AX), lax.axis_index(AZ), lax.axis_index(AY)]).astype(jnp.int32)
     doc_col = jnp.broadcast_to(doc_ids[0][:, None], (TOK, HEAD_SIZE))
     doc_row = jnp.broadcast_to(doc_ids, (8, TOK))
-    some = forward_pass(q, k, v, og, doc_col, doc_row, 0, 2)
-    *some, both = lax.optimization_barrier((*some, both))
-    weight = lax.all_gather(both, (AX, AZ), tiled=True)
-    context, term = forward_pass(q, k, v, og, doc_col, doc_row, 2, 2, some)
+    first = gather_first(shard)
+    done = forward_pass(q, k, v, og, doc_col, doc_row, 0, 1)
+    first, done = lax.optimization_barrier((first, done))
+    second = gather_second(*first)
+    done = forward_pass(q, k, v, og, doc_col, doc_row, 1, 2, done)
+    second, done = lax.optimization_barrier((second, done))
+    parts = gather_last(first[0], *second)
+    context, term = forward_pass(q, k, v, og, doc_col, doc_row, 3, 1, done)
     pair = lax.psum_scatter(term, (AX, AZ), scatter_dimension=0, tiled=True)
     block_out, query_grad, key_grad, value_grad = backward_pass(
-        q, k, v, og, context, residual_in[0], doc_col, doc_row, weight
+        pos, q, k, v, og, context, residual_in[0], doc_col, doc_row, parts
     )
     pair, query_grad = lax.optimization_barrier((pair, query_grad))
     sent = jnp.where(y == 0, pair[SHARD:], pair[:SHARD])

time: 245 us -> 238 us (0.971)
  waiting for transfers between devices: 156 us -> 83.3 us
  starting transfers between devices: 5.31 us -> 55.6 us
  Pallas kernels: 60.9 us -> 70.6 us
  local copies, waits for them, and re-layouts: 1.4 us -> 6.2 us
    all_gather x1 -> x0, waiting for transfers between devices: 82.7 us -> none  [on_device(): weight = lax.all_gather(both, (AX, AZ), tiled=True)]
    ppermute x0 -> x28, waiting for transfers between devices: none -> 70.3 us  [from_(): lax.ppermute(block, axis, [(i, (i - distance) % count) for i in range(cou...]
    reduce_scatter x1, waiting for transfers between devices: 63.1 us -> 6.65 us  [on_device(): pair = lax.psum_scatter(term, (AX, AZ), scatter_dimension=0, tiled=True)]
    ppermute x0 -> x28, starting transfers between devices: none -> 35.5 us  [from_(): lax.ppermute(block, axis, [(i, (i - distance) % count) for i in range(cou...]
    ppermute x3 -> x2, starting transfers between devices: 5.23 us -> 20.1 us  [swapped(): lax.ppermute(block, axis, [(i, i ^ 1 << distance) for i in range(count)])]
    pallas_call x1, Pallas kernels: 36 us -> 42.2 us  [backward_pass(): pl.pallas_call(functools.partial(backward_kernel, places), out_shape=[jax...]
    pallas_call x2 -> x3, Pallas kernels: 24.9 us -> 28.3 us  [forward_pass(): pl.pallas_call(forward_kernel, out_shape=[jax.ShapeDtypeStruct((TOK, WIDT...]
    ppermute x3 -> x2, waiting for transfers between devices: 9.78 us -> 6.35 us  [swapped(): lax.ppermute(block, axis, [(i, i ^ 1 << distance) for i in range(count)])]
  transfers between devices with their start and end apart: 5 -> 31, of which waited for: 4 -> 14; matrix products, arithmetic and copies ran while one was open for 1% -> 2% of each run, Pallas kernels for 25% -> 26%
where the time goes in v2:
time: 238 us
  waiting for transfers between devices  83.3 us (35%)
  Pallas kernels  70.6 us (30%)
  starting transfers between devices  55.6 us (23%)
  between operations  15 us (6%)
  other arithmetic  7.08 us (3%)
  local copies, waits for them, and re-layouts  6.2 us (3%)
    ppermute x28, waiting for transfers between devices, from_(): lax.ppermute(block, axis, [(i, (i - distance) % count) for i in range(cou...  70.3 us
    pallas_call x1, Pallas kernels, backward_pass(): pl.pallas_call(functools.partial(backward_kernel, places), out_shape=[jax...  42.2 us
    ppermute x28, starting transfers between devices, from_(): lax.ppermute(block, axis, [(i, (i - distance) % count) for i in range(cou...  35.5 us
    pallas_call x3, Pallas kernels, forward_pass(): pl.pallas_call(forward_kernel, out_shape=[jax.ShapeDtypeStruct((TOK, WIDT...  28.3 us
    ppermute x2, starting transfers between devices, swapped(): lax.ppermute(block, axis, [(i, i ^ 1 << distance) for i in range(count)])  20.1 us
    reduce_scatter x1, waiting for transfers between devices, on_device(): pair = lax.psum_scatter(term, (AX, AZ), scatter_dimension=0, tiled=True)  6.65 us
    ppermute x2, waiting for transfers between devices, swapped(): lax.ppermute(block, axis, [(i, i ^ 1 << distance) for i in range(count)])  6.35 us
  transfers between devices with their start and end apart: 31, of which 14 were waited for; matrix products, arithmetic and copies ran while one was open for 2% of the time, Pallas kernels for 26%

profile of v2, /device:TPU:1, one launch (start us, length us, event | category | flops | bytes accessed | tf_op | source)
XLA Modules:
  0.0 237.7 jit_solution(12767387008941483053)
XLA Ops:
  7.2 1.0 fusion.3
  8.2 3.4 %collective-permute-start.2 = (bf16[1,32,2560]{2,1,0:T(8,128)(2,1)S(1)}, bf16[1,32,2560]{2,1,0:T(8,128)(2,1)S(1)}, u32[]{:S(2)}, u32[]{:S(2)}) collective-permute-start(bf16[1,32,2560]{2,1,0:T(8,128)(2,1)S(1)} %get-tuple-element.64), channel_id=1, source_target_pairs={{0,24},{8,0},{16,8},{24,16},{1,25},{9,1},{17,9},{25,17},{2,26},{10... | collective-permute-start | bytes 491528 | tf_op jit(solution)/shard_map/ppermute | solution.py:40
  12.7 1.3 collective-permute-start.6
  14.0 0.9 slice.39
  15.1 0.7 reduce
  15.8 0.8 broadcast_in_dim.34.doc_col
  17.2 7.9 %attend_forward.3 = (bf16[384,2560]{1,0:T(8,128)(2,1)}, bf16[2560,2560]{1,0:T(8,128)(2,1)}) custom-call(bf16[384,2560]{1,0:T(8,128)(2,1)} %bitcast.29, bf16[384,2560]{1,0:T(8,128)(2,1)} %bitcast.33, bf16[384,2560]{1,0:T(8,128)(2,1)} %bitcast.37, bf16[384,2560]{1,0:T(8,128)(2,1)} %bitcast.41, s32[384,128]{1,0:T(8,128)} %broadcast_in_dim.34.doc_col, ...), custom_call_target="tpu_custom_call" | custom-call | flops 1650000000 | bytes 6000000 | tf_op jit(solution)/shard_map/attend_forward/pallas_call | solution.py:134
  25.3 3.8 %collective-permute-start.10 = (bf16[2,32,2560]{2,1,0:T(8,128)(2,1)S(1)}, bf16[2,32,2560]{2,1,0:T(8,128)(2,1)S(1)}, u32[]{:S(2)}, u32[]{:S(2)}) collective-permute-start(bf16[2,32,2560]{2,1,0:T(8,128)(2,1)S(1)} %pad_maximum_fusion.3), channel_id=1, source_target_pairs={{0,6},{2,0},{4,2},{6,4},{1,7},{3,1},{5,3},{7,5},{8,14},{10,8},{12,... | collective-permute-start | bytes 983048 | tf_op jit(solution)/shard_map/ppermute | solution.py:40
  29.1 2.1 collective-permute-start.7
  31.2 1.2 collective-permute-start.8
  32.4 12.4 %attend_forward.4 = (bf16[384,2560]{1,0:T(8,128)(2,1)}, bf16[2560,2560]{1,0:T(8,128)(2,1)}) custom-call(bf16[384,2560]{1,0:T(8,128)(2,1)} %bitcast.30, bf16[384,2560]{1,0:T(8,128)(2,1)} %bitcast.34, bf16[384,2560]{1,0:T(8,128)(2,1)} %bitcast.38, bf16[384,2560]{1,0:T(8,128)(2,1)} %bitcast.42, ...), custom_call_target="tpu_custom_call", output_to_operand_aliasing={{0}: (6, {}), {1}: (7, {})} | custom-call | flops 3300000000 | bytes 12000000 | tf_op jit(solution)/shard_map/attend_forward/pallas_call | solution.py:134
  44.9 0.8 collective-permute-start.12
  45.6 1.3 collective-permute-start.13
  47.0 5.4 %collective-permute-done.12 = bf16[2,32,2560]{2,1,0:T(8,128)(2,1)S(1)} collective-permute-done((bf16[2,32,2560]{2,1,0:T(8,128)(2,1)S(1)}, bf16[2,32,2560]{2,1,0:T(8,128)(2,1)S(1)}, u32[]{:S(2)}, u32[]{:S(2)}) %collective-permute-start.12) | collective-permute-done | bytes 327712 | tf_op jit(solution)/shard_map/ppermute | solution.py:40
  52.6 5.8 %collective-permute-done.13.refs_11_ = bf16[4,32,2560]{2,1,0:T(8,128)(2,1)S(1)} collective-permute-done((bf16[4,32,2560]{2,1,0:T(8,128)(2,1)S(1)}, bf16[4,32,2560]{2,1,0:T(8,128)(2,1)S(1)}, u32[]{:S(2)}, u32[]{:S(2)}) %collective-permute-start.13) | collective-permute-done | bytes 655392 | tf_op jit(solution)/shard_map/ppermute | solution.py:40
  58.4 0.9 copy-done.10
  59.2 8.0 %attend_forward.5 = (bf16[384,2560]{1,0:T(8,128)(2,1)}, bf16[2560,2560]{1,0:T(8,128)(2,1)}) custom-call(bf16[384,2560]{1,0:T(8,128)(2,1)} %bitcast.31, bf16[384,2560]{1,0:T(8,128)(2,1)} %bitcast.35, bf16[384,2560]{1,0:T(8,128)(2,1)} %bitcast.39, bf16[384,2560]{1,0:T(8,128)(2,1)} %bitcast.43, ...), custom_call_target="tpu_custom_call", output_to_operand_aliasing={{0}: (6, {}), {1}: (7, {})} | custom-call | flops 1650000000 | bytes 6000000 | tf_op jit(solution)/shard_map/attend_forward/pallas_call | solution.py:134
  67.3 2.4 %collective-permute-start.18 = (bf16[8,32,2560]{2,1,0:T(8,128)(2,1)S(1)}, bf16[8,32,2560]{2,1,0:T(8,128)(2,1)S(1)}, u32[]{:S(2)}, u32[]{:S(2)}) collective-permute-start(bf16[8,32,2560]{2,1,0:T(8,128)(2,1)S(1)} %pad_maximum_fusion.refs_5_), channel_id=1, source_target_pairs={{0,24},{8,0},{16,8},{24,16},{1,25},{9,1},{17,9},{25,17},{2,26},{10... | collective-permute-start | bytes 3932168 | tf_op jit(solution)/shard_map/ppermute | solution.py:40
  69.7 2.3 collective-permute-start.22
  72.1 9.8 %collective-permute-done.22.refs_12_ = bf16[4,32,2560]{2,1,0:T(8,128)(2,1)S(1)} collective-permute-done((bf16[4,32,2560]{2,1,0:T(8,128)(2,1)S(1)}, bf16[4,32,2560]{2,1,0:T(8,128)(2,1)S(1)}, u32[]{:S(2)}, u32[]{:S(2)}) %collective-permute-start.22) | collective-permute-done | bytes 655392 | tf_op jit(solution)/shard_map/ppermute | solution.py:40
  81.9 2.9 %collective-permute-start.26 = (bf16[2,32,2560]{2,1,0:T(8,128)(2,1)S(1)}, bf16[2,32,2560]{2,1,0:T(8,128)(2,1)S(1)}, u32[]{:S(2)}, u32[]{:S(2)}) collective-permute-start(bf16[2,32,2560]{2,1,0:T(8,128)(2,1)S(1)} %slice.53), channel_id=1, source_target_pairs={{0,6},{2,0},{4,2},{6,4},{1,7},{3,1},{5,3},{7,5},{8,14},{10,8},{12,... | collective-permute-start | bytes 983048 | tf_op jit(solution)/shard_map/ppermute | solution.py:40
  84.9 1.0 slice.54
  85.9 2.7 %collective-permute-start.14 = (bf16[8,16,2560]{2,1,0:T(8,128)(2,1)S(1)}, bf16[8,16,2560]{2,1,0:T(8,128)(2,1)S(1)}, u32[]{:S(2)}, u32[]{:S(2)}) collective-permute-start(bf16[8,16,2560]{2,1,0:T(8,128)(2,1)S(1)} %pad_maximum_fusion.2.refs_0_), channel_id=1, source_target_pairs={{0,6},{2,0},{4,2},{6,4},{1,7},{3,1},{5,3},{7,5},{8,14},{10,8},{12,... | collective-permute-start | bytes 1966088 | tf_op jit(solution)/shard_map/ppermute | solution.py:40
  88.6 10.8 %collective-permute-done.26.refs_16_ = bf16[2,32,2560]{2,1,0:T(8,128)(2,1)S(1)} collective-permute-done((bf16[2,32,2560]{2,1,0:T(8,128)(2,1)S(1)}, bf16[2,32,2560]{2,1,0:T(8,128)(2,1)S(1)}, u32[]{:S(2)}, u32[]{:S(2)}) %collective-permute-start.26) | collective-permute-done | bytes 327712 | tf_op jit(solution)/shard_map/ppermute | solution.py:40
  99.4 4.3 %collective-permute-done.28.refs_18_ = bf16[2,32,2560]{2,1,0:T(8,128)(2,1)S(1)} collective-permute-done((bf16[2,32,2560]{2,1,0:T(8,128)(2,1)S(1)}, bf16[2,32,2560]{2,1,0:T(8,128)(2,1)S(1)}, u32[]{:S(2)}, u32[]{:S(2)}) %collective-permute-start.28) | collective-permute-done | bytes 327712 | tf_op jit(solution)/shard_map/ppermute | solution.py:40
  103.7 1.3 collective-permute-start.27
  105.0 0.8 collective-permute-start.23
  105.9 6.5 %collective-permute-done.19.refs_7_ = bf16[8,32,2560]{2,1,0:T(8,128)(2,1)S(1)} collective-permute-done((bf16[8,32,2560]{2,1,0:T(8,128)(2,1)S(1)}, bf16[8,32,2560]{2,1,0:T(8,128)(2,1)S(1)}, u32[]{:S(2)}, u32[]{:S(2)}) %collective-permute-start.19) | collective-permute-done | bytes 1310752 | tf_op jit(solution)/shard_map/ppermute | solution.py:40
  112.4 1.4 collective-permute-start.29
  114.0 10.5 %collective-permute-done.14.refs_1_ = bf16[8,16,2560]{2,1,0:T(8,128)(2,1)S(1)} collective-permute-done((bf16[8,16,2560]{2,1,0:T(8,128)(2,1)S(1)}, bf16[8,16,2560]{2,1,0:T(8,128)(2,1)S(1)}, u32[]{:S(2)}, u32[]{:S(2)}) %collective-permute-start.14) | collective-permute-done | bytes 655392 | tf_op jit(solution)/shard_map/ppermute | solution.py:40
  124.5 1.5 collective-permute-start.20
  126.3 3.2 %collective-permute-start.21 = (bf16[4,32,2560]{2,1,0:T(8,128)(2,1)S(1)}, bf16[4,32,2560]{2,1,0:T(8,128)(2,1)S(1)}, u32[]{:S(2)}, u32[]{:S(2)}) collective-permute-start(bf16[4,32,2560]{2,1,0:T(8,128)(2,1)S(1)} %slice.52), channel_id=1, source_target_pairs={{0,8},{8,16},{16,24},{24,0},{1,9},{9,17},{17,25},{25,1},{2,10},{10... | collective-permute-start | bytes 1966088 | tf_op jit(solution)/shard_map/ppermute | solution.py:40
  129.7 1.4 collective-permute-start.17
  131.2 0.7 pad_add_fusion.pos
  131.9 13.7 %collective-permute-done.16.refs_3_ = bf16[4,16,2560]{2,1,0:T(8,128)(2,1)} collective-permute-done((bf16[4,16,2560]{2,1,0:T(8,128)(2,1)S(1)}, bf16[4,16,2560]{2,1,0:T(8,128)(2,1)}, u32[]{:S(2)}, u32[]{:S(2)}) %collective-permute-start.16) | collective-permute-done | bytes 327712 | tf_op jit(solution)/shard_map/ppermute | solution.py:40
  145.6 2.5 %collective-permute-done.17.refs_4_ = bf16[4,16,2560]{2,1,0:T(8,128)(2,1)} collective-permute-done((bf16[4,16,2560]{2,1,0:T(8,128)(2,1)S(1)}, bf16[4,16,2560]{2,1,0:T(8,128)(2,1)}, u32[]{:S(2)}, u32[]{:S(2)}) %collective-permute-start.17) | collective-permute-done | bytes 327712 | tf_op jit(solution)/shard_map/ppermute | solution.py:40
  148.1 0.6 collective-permute-done.21.refs_9_
  148.7 0.8 copy-done.12
  149.5 42.2 %attend_backward.1 = (bf16[384,2560]{1,0:T(8,128)(2,1)}, bf16[384,2560]{1,0:T(8,128)(2,1)}, bf16[384,2560]{1,0:T(8,128)(2,1)}, bf16[384,2560]{1,0:T(8,128)(2,1)}) custom-call(s32[3]{0:T(128)} %pad_add_fusion.pos, bf16[384,2560]{1,0:T(8,128)(2,1)} %bitcast.32, bf16[384,2560]{1,0:T(8,128)(2,1)} %bitcast.36, bf16[384,2560]{1,0:T(8,128)(2,1)} %bitcast.40, ...), custom_call_target="tpu_custom_call" | custom-call | flops 14000000000 | bytes 35000000 | tf_op jit(solution)/shard_map/attend_backward/pallas_call | solution.py:203
  191.8 6.6 %reduce-scatter.2.cloned.1.call-done = bf16[160,2560]{1,0:T(8,128)(2,1)} async-done(((bf16[2560,2560]{1,0:T(8,128)(2,1)}), bf16[160,2560]{1,0:T(8,128)(2,1)}) %reduce-scatter.2.cloned.1.call-update) | async-done | bytes 819216 | tf_op jit(solution)/shard_map/reduce_scatter | solution.py:242
  198.4 1.2 broadcast_select_fusion
  199.6 1.4 collective-permute-start.30
  201.6 4.8 %collective-permute-done.30 = bf16[80,2560]{1,0:T(8,128)(2,1)S(1)} collective-permute-done((bf16[80,2560]{1,0:T(8,128)(2,1)S(1)}, bf16[80,2560]{1,0:T(8,128)(2,1)S(1)}, u32[]{:S(2)}, u32[]{:S(2)}) %collective-permute-start.30) | collective-permute-done | bytes 409632 | tf_op jit(solution)/shard_map/ppermute | solution.py:32
  206.5 2.3 fusion.2
  208.8 20.2 %conditional.4 = (bf16[80,2560]{1,0:T(8,128)(2,1)}) conditional(s32[]{:T(128)} %clamp.3, bf16[80,2560]{1,0:T(8,128)(2,1)S(1)} %get-tuple-element.62, bf16[80,2560]{1,0:T(8,128)(2,1)S(1)} %get-tuple-element.62), branch_computations={%region_1.2_spmd, %region_2.3_spmd} | conditional | bytes 1638448
  208.8 18.7 %collective-permute-start = (bf16[80,2560]{1,0:T(8,128)(2,1)S(1)}, bf16[80,2560]{1,0:T(8,128)(2,1)}, u32[]{:S(2)}, u32[]{:S(2)}) collective-permute-start(bf16[80,2560]{1,0:T(8,128)(2,1)S(1)} %param), channel_id=1, source_target_pairs={{0,32},{32,0},{64,96},{96,64},{1,33},{33,1},{65,97},{97,65},{2,34}... | collective-permute-start | bytes 1228808 | tf_op jit(solution)/shard_map/cond/branch_0_fun/ppermute | solution.py:32
  227.5 1.5 collective-permute-done
  229.0 1.9 fusion.1
  (74 shorter events, 3.4 us)
Async XLA Ops:
  7.2 191.2 %reduce-scatter.2.cloned.1.call-start = ((), (), s32[]{:S(2)}) async-start(), calls=%async_computation.1 | async-start | bytes 13926400 | tf_op jit(solution)/shard_map/reduce_scatter | solution.py:242
  8.2 16.9 %collective-permute-start.2 = (bf16[1,32,2560]{2,1,0:T(8,128)(2,1)S(1)}, bf16[1,32,2560]{2,1,0:T(8,128)(2,1)S(1)}, u32[]{:S(2)}, u32[]{:S(2)}) collective-permute-start(bf16[1,32,2560]{2,1,0:T(8,128)(2,1)S(1)} %get-tuple-element.64), channel_id=1, source_target_pairs={{0,24},{8,0},{16,8},{24,16},{1,25},{9,1},{17,9},{25,17},{2,26},{10... | collective-permute-start | bytes 491528 | tf_op jit(solution)/shard_map/ppermute | solution.py:40
  11.6 13.5 %collective-permute-start.3 = (bf16[1,32,2560]{2,1,0:T(8,128)(2,1)S(1)}, bf16[1,32,2560]{2,1,0:T(8,128)(2,1)S(1)}, u32[]{:S(2)}, u32[]{:S(2)}) collective-permute-start(bf16[1,32,2560]{2,1,0:T(8,128)(2,1)S(1)} %get-tuple-element.64), channel_id=1, source_target_pairs={{0,16},{8,24},{16,0},{24,8},{1,17},{9,25},{17,1},{25,9},{2,18},{10... | collective-permute-start | bytes 491528 | tf_op jit(solution)/shard_map/ppermute | solution.py:40
  12.1 13.0 %collective-permute-start.4 = (bf16[1,32,2560]{2,1,0:T(8,128)(2,1)S(1)}, bf16[1,32,2560]{2,1,0:T(8,128)(2,1)S(1)}, u32[]{:S(2)}, u32[]{:S(2)}) collective-permute-start(bf16[1,32,2560]{2,1,0:T(8,128)(2,1)S(1)} %get-tuple-element.64), channel_id=1, source_target_pairs={{0,8},{8,16},{16,24},{24,0},{1,9},{9,17},{17,25},{25,1},{2,10},{10... | collective-permute-start | bytes 491528 | tf_op jit(solution)/shard_map/ppermute | solution.py:40
  12.7 12.4 %collective-permute-start.6 = (bf16[1,32,2560]{2,1,0:T(8,128)(2,1)S(1)}, bf16[1,32,2560]{2,1,0:T(8,128)(2,1)S(1)}, u32[]{:S(2)}, u32[]{:S(2)}) collective-permute-start(bf16[1,32,2560]{2,1,0:T(8,128)(2,1)S(1)} %get-tuple-element.63), channel_id=1, source_target_pairs={{0,1},{1,0},{2,3},{3,2},{4,5},{5,4},{6,7},{7,6},{8,9},{9,8},{10,11... | collective-permute-start | bytes 491528 | tf_op jit(solution)/shard_map/ppermute | solution.py:40
  14.9 10.1 %collective-permute-start.5 = (bf16[1,16,2560]{2,1,0:T(8,128)(2,1)S(1)}, bf16[1,16,2560]{2,1,0:T(8,128)(2,1)S(1)}, u32[]{:S(2)}, u32[]{:S(2)}) collective-permute-start(bf16[1,16,2560]{2,1,0:T(8,128)(2,1)S(1)} %slice.39), channel_id=1, source_target_pairs={{0,1},{1,0},{2,3},{3,2},{4,5},{5,4},{6,7},{7,6},{8,9},{9,8},{10,11... | collective-permute-start | bytes 245768 | tf_op jit(solution)/shard_map/ppermute | solution.py:40
  25.3 46.7 %copy-start.3 = (bf16[4,32,2560]{2,1,0:T(8,128)(2,1)}, bf16[4,32,2560]{2,1,0:T(8,128)(2,1)S(1)}, u32[]{:S(2)}) copy-start(bf16[4,32,2560]{2,1,0:T(8,128)(2,1)S(1)} %pad_maximum_fusion.1.refs_10_) | copy-start | bytes 1966084
  25.3 21.7 %collective-permute-start.10 = (bf16[2,32,2560]{2,1,0:T(8,128)(2,1)S(1)}, bf16[2,32,2560]{2,1,0:T(8,128)(2,1)S(1)}, u32[]{:S(2)}, u32[]{:S(2)}) collective-permute-start(bf16[2,32,2560]{2,1,0:T(8,128)(2,1)S(1)} %pad_maximum_fusion.3), channel_id=1, source_target_pairs={{0,6},{2,0},{4,2},{6,4},{1,7},{3,1},{5,3},{7,5},{8,14},{10,8},{12,... | collective-permute-start | bytes 983048 | tf_op jit(solution)/shard_map/ppermute | solution.py:40
  29.1 17.9 %collective-permute-start.11 = (bf16[2,32,2560]{2,1,0:T(8,128)(2,1)S(1)}, bf16[2,32,2560]{2,1,0:T(8,128)(2,1)S(1)}, u32[]{:S(2)}, u32[]{:S(2)}) collective-permute-start(bf16[2,32,2560]{2,1,0:T(8,128)(2,1)S(1)} %pad_maximum_fusion.3), channel_id=1, source_target_pairs={{0,4},{2,6},{4,0},{6,2},{1,5},{3,7},{5,1},{7,3},{8,12},{10,14},{12... | collective-permute-start | bytes 983048 | tf_op jit(solution)/shard_map/ppermute | solution.py:40
  29.1 15.8 %collective-permute-start.7 = (bf16[2,16,2560]{2,1,0:T(8,128)(2,1)S(1)}, bf16[2,16,2560]{2,1,0:T(8,128)(2,1)S(1)}, u32[]{:S(2)}, u32[]{:S(2)}) collective-permute-start(bf16[2,16,2560]{2,1,0:T(8,128)(2,1)S(1)} %pad_maximum_fusion.4), channel_id=1, source_target_pairs={{0,24},{8,0},{16,8},{24,16},{1,25},{9,1},{17,9},{25,17},{2,26},{10... | collective-permute-start | bytes 491528 | tf_op jit(solution)/shard_map/ppermute | solution.py:40
  31.2 14.4 %collective-permute-start.8 = (bf16[2,16,2560]{2,1,0:T(8,128)(2,1)S(1)}, bf16[2,16,2560]{2,1,0:T(8,128)(2,1)S(1)}, u32[]{:S(2)}, u32[]{:S(2)}) collective-permute-start(bf16[2,16,2560]{2,1,0:T(8,128)(2,1)S(1)} %pad_maximum_fusion.4), channel_id=1, source_target_pairs={{0,16},{8,24},{16,0},{24,8},{1,17},{9,25},{17,1},{25,9},{2,18},{10... | collective-permute-start | bytes 491528 | tf_op jit(solution)/shard_map/ppermute | solution.py:40
  32.4 14.5 %collective-permute-start.9 = (bf16[2,16,2560]{2,1,0:T(8,128)(2,1)S(1)}, bf16[2,16,2560]{2,1,0:T(8,128)(2,1)S(1)}, u32[]{:S(2)}, u32[]{:S(2)}) collective-permute-start(bf16[2,16,2560]{2,1,0:T(8,128)(2,1)S(1)} %pad_maximum_fusion.4), channel_id=1, source_target_pairs={{0,8},{8,16},{16,24},{24,0},{1,9},{9,17},{17,25},{25,1},{2,10},{10... | collective-permute-start | bytes 491528 | tf_op jit(solution)/shard_map/ppermute | solution.py:40
  44.9 7.6 %collective-permute-start.12 = (bf16[2,32,2560]{2,1,0:T(8,128)(2,1)S(1)}, bf16[2,32,2560]{2,1,0:T(8,128)(2,1)S(1)}, u32[]{:S(2)}, u32[]{:S(2)}) collective-permute-start(bf16[2,32,2560]{2,1,0:T(8,128)(2,1)S(1)} %pad_maximum_fusion.3), channel_id=1, source_target_pairs={{0,2},{2,4},{4,6},{6,0},{1,3},{3,5},{5,7},{7,1},{8,10},{10,12},{12... | collective-permute-start | bytes 983048 | tf_op jit(solution)/shard_map/ppermute | solution.py:40
  45.6 12.7 %collective-permute-start.13 = (bf16[4,32,2560]{2,1,0:T(8,128)(2,1)S(1)}, bf16[4,32,2560]{2,1,0:T(8,128)(2,1)S(1)}, u32[]{:S(2)}, u32[]{:S(2)}) collective-permute-start(bf16[4,32,2560]{2,1,0:T(8,128)(2,1)S(1)} %pad_maximum_fusion.1.refs_10_), channel_id=1, source_target_pairs={{0,1},{1,0},{2,3},{3,2},{4,5},{5,4},{6,7},{7,6},{8,9},{9,8},{10,11... | collective-permute-start | bytes 1966088 | tf_op jit(solution)/shard_map/ppermute | solution.py:40
  47.0 52.4 %copy-start.4 = (bf16[8,16,2560]{2,1,0:T(8,128)(2,1)}, bf16[8,16,2560]{2,1,0:T(8,128)(2,1)S(1)}, u32[]{:S(2)}) copy-start(bf16[8,16,2560]{2,1,0:T(8,128)(2,1)S(1)} %pad_maximum_fusion.2.refs_0_) | copy-start | bytes 1966084
  52.6 19.4 %copy-start.1 = (bf16[8,32,2560]{2,1,0:T(8,128)(2,1)}, bf16[8,32,2560]{2,1,0:T(8,128)(2,1)S(1)}, u32[]{:S(2)}) copy-start(bf16[8,32,2560]{2,1,0:T(8,128)(2,1)S(1)} %pad_maximum_fusion.refs_5_) | copy-start | bytes 3932164
  58.4 0.9 copy-start.10
  67.3 37.8 %collective-permute-start.18 = (bf16[8,32,2560]{2,1,0:T(8,128)(2,1)S(1)}, bf16[8,32,2560]{2,1,0:T(8,128)(2,1)S(1)}, u32[]{:S(2)}, u32[]{:S(2)}) collective-permute-start(bf16[8,32,2560]{2,1,0:T(8,128)(2,1)S(1)} %pad_maximum_fusion.refs_5_), channel_id=1, source_target_pairs={{0,24},{8,0},{16,8},{24,16},{1,25},{9,1},{17,9},{25,17},{2,26},{10... | collective-permute-start | bytes 3932168 | tf_op jit(solution)/shard_map/ppermute | solution.py:40
  69.7 12.2 %collective-permute-start.22 = (bf16[4,32,2560]{2,1,0:T(8,128)(2,1)S(1)}, bf16[4,32,2560]{2,1,0:T(8,128)(2,1)S(1)}, u32[]{:S(2)}, u32[]{:S(2)}) collective-permute-start(bf16[4,32,2560]{2,1,0:T(8,128)(2,1)S(1)} %pad_maximum_fusion.1.refs_10_), channel_id=1, source_target_pairs={{0,6},{2,0},{4,2},{6,4},{1,7},{3,1},{5,3},{7,5},{8,14},{10,8},{12,... | collective-permute-start | bytes 1966088 | tf_op jit(solution)/shard_map/ppermute | solution.py:40
  72.0 12.9 %collective-permute-start.24 = (bf16[4,32,2560]{2,1,0:T(8,128)(2,1)S(1)}, bf16[4,32,2560]{2,1,0:T(8,128)(2,1)}, u32[]{:S(2)}, u32[]{:S(2)}) collective-permute-start(bf16[4,32,2560]{2,1,0:T(8,128)(2,1)S(1)} %pad_maximum_fusion.1.refs_10_), channel_id=1, source_target_pairs={{0,2},{2,4},{4,6},{6,0},{1,3},{3,5},{5,7},{7,1},{8,10},{10,12},{12... | collective-permute-start | bytes 1966088 | tf_op jit(solution)/shard_map/ppermute | solution.py:40
  72.0 40.3 %collective-permute-start.19 = (bf16[8,32,2560]{2,1,0:T(8,128)(2,1)S(1)}, bf16[8,32,2560]{2,1,0:T(8,128)(2,1)S(1)}, u32[]{:S(2)}, u32[]{:S(2)}) collective-permute-start(bf16[8,32,2560]{2,1,0:T(8,128)(2,1)S(1)} %pad_maximum_fusion.refs_5_), channel_id=1, source_target_pairs={{0,8},{8,16},{16,24},{24,0},{1,9},{9,17},{17,25},{25,1},{2,10},{10... | collective-permute-start | bytes 3932168 | tf_op jit(solution)/shard_map/ppermute | solution.py:40
  81.9 31.9 %copy-start.7 = (bf16[4,32,2560]{2,1,0:T(8,128)(2,1)}, bf16[4,32,2560]{2,1,0:T(8,128)(2,1)S(1)}, u32[]{:S(2)}) copy-start(bf16[4,32,2560]{2,1,0:T(8,128)(2,1)S(1)} %collective-permute-done.22.refs_12_) | copy-start | bytes 1966084
  81.9 17.5 %collective-permute-start.26 = (bf16[2,32,2560]{2,1,0:T(8,128)(2,1)S(1)}, bf16[2,32,2560]{2,1,0:T(8,128)(2,1)S(1)}, u32[]{:S(2)}, u32[]{:S(2)}) collective-permute-start(bf16[2,32,2560]{2,1,0:T(8,128)(2,1)S(1)} %slice.53), channel_id=1, source_target_pairs={{0,6},{2,0},{4,2},{6,4},{1,7},{3,1},{5,3},{7,5},{8,14},{10,8},{12,... | collective-permute-start | bytes 983048 | tf_op jit(solution)/shard_map/ppermute | solution.py:40
  85.9 17.8 %collective-permute-start.28 = (bf16[2,32,2560]{2,1,0:T(8,128)(2,1)S(1)}, bf16[2,32,2560]{2,1,0:T(8,128)(2,1)S(1)}, u32[]{:S(2)}, u32[]{:S(2)}) collective-permute-start(bf16[2,32,2560]{2,1,0:T(8,128)(2,1)S(1)} %slice.54), channel_id=1, source_target_pairs={{0,2},{2,4},{4,6},{6,0},{1,3},{3,5},{5,7},{7,1},{8,10},{10,12},{12... | collective-permute-start | bytes 983048 | tf_op jit(solution)/shard_map/ppermute | solution.py:40
  85.9 38.5 %collective-permute-start.14 = (bf16[8,16,2560]{2,1,0:T(8,128)(2,1)S(1)}, bf16[8,16,2560]{2,1,0:T(8,128)(2,1)S(1)}, u32[]{:S(2)}, u32[]{:S(2)}) collective-permute-start(bf16[8,16,2560]{2,1,0:T(8,128)(2,1)S(1)} %pad_maximum_fusion.2.refs_0_), channel_id=1, source_target_pairs={{0,6},{2,0},{4,2},{6,4},{1,7},{3,1},{5,3},{7,5},{8,14},{10,8},{12,... | collective-permute-start | bytes 1966088 | tf_op jit(solution)/shard_map/ppermute | solution.py:40
  99.4 49.3 %copy-start.13 = (bf16[2,32,2560]{2,1,0:T(8,128)(2,1)}, bf16[2,32,2560]{2,1,0:T(8,128)(2,1)S(1)}, u32[]{:S(2)}) copy-start(bf16[2,32,2560]{2,1,0:T(8,128)(2,1)S(1)} %collective-permute-done.26.refs_16_) | copy-start | bytes 983044
  99.4 27.0 %collective-permute-start.15 = (bf16[8,16,2560]{2,1,0:T(8,128)(2,1)S(1)}, bf16[8,16,2560]{2,1,0:T(8,128)(2,1)S(1)}, u32[]{:S(2)}, u32[]{:S(2)}) collective-permute-start(bf16[8,16,2560]{2,1,0:T(8,128)(2,1)S(1)} %pad_maximum_fusion.2.refs_0_), channel_id=1, source_target_pairs={{0,2},{2,4},{4,6},{6,0},{1,3},{3,5},{5,7},{7,1},{8,10},{10,12},{12... | collective-permute-start | bytes 1966088 | tf_op jit(solution)/shard_map/ppermute | solution.py:40
  103.7 27.5 %copy-start.14 = (bf16[2,32,2560]{2,1,0:T(8,128)(2,1)}, bf16[2,32,2560]{2,1,0:T(8,128)(2,1)S(1)}, u32[]{:S(2)}) copy-start(bf16[2,32,2560]{2,1,0:T(8,128)(2,1)S(1)} %collective-permute-done.28.refs_18_) | copy-start | bytes 983044
  103.7 10.1 %collective-permute-start.27 = (bf16[2,32,2560]{2,1,0:T(8,128)(2,1)S(1)}, bf16[2,32,2560]{2,1,0:T(8,128)(2,1)S(1)}, u32[]{:S(2)}, u32[]{:S(2)}) collective-permute-start(bf16[2,32,2560]{2,1,0:T(8,128)(2,1)S(1)} %collective-permute-done.26.refs_16_), channel_id=1, source_target_pairs={{0,1},{1,0},{2,3},{3,2},{4,5},{5,4},{6,7},{7,6},{8,9},{9,8},{10,11... | collective-permute-start | bytes 983048 | tf_op jit(solution)/shard_map/ppermute | solution.py:40
  105.0 24.6 %copy-start.5 = (bf16[8,32,2560]{2,1,0:T(8,128)(2,1)}, bf16[8,32,2560]{2,1,0:T(8,128)(2,1)S(1)}, u32[]{:S(2)}) copy-start(bf16[8,32,2560]{2,1,0:T(8,128)(2,1)S(1)} %collective-permute-done.18.refs_6_) | copy-start | bytes 3932164
  105.0 24.7 %collective-permute-start.23 = (bf16[4,32,2560]{2,1,0:T(8,128)(2,1)S(1)}, bf16[4,32,2560]{2,1,0:T(8,128)(2,1)S(1)}, u32[]{:S(2)}, u32[]{:S(2)}) collective-permute-start(bf16[4,32,2560]{2,1,0:T(8,128)(2,1)S(1)} %collective-permute-done.22.refs_12_), channel_id=1, source_target_pairs={{0,1},{1,0},{2,3},{3,2},{4,5},{5,4},{6,7},{7,6},{8,9},{9,8},{10,11... | collective-permute-start | bytes 1966088 | tf_op jit(solution)/shard_map/ppermute | solution.py:40
  112.4 17.3 %copy-start.6 = (bf16[8,32,2560]{2,1,0:T(8,128)(2,1)}, bf16[8,32,2560]{2,1,0:T(8,128)(2,1)S(1)}, u32[]{:S(2)}) copy-start(bf16[8,32,2560]{2,1,0:T(8,128)(2,1)S(1)} %collective-permute-done.19.refs_7_) | copy-start | bytes 3932164
  112.4 17.2 %collective-permute-start.29 = (bf16[2,32,2560]{2,1,0:T(8,128)(2,1)S(1)}, bf16[2,32,2560]{2,1,0:T(8,128)(2,1)S(1)}, u32[]{:S(2)}, u32[]{:S(2)}) collective-permute-start(bf16[2,32,2560]{2,1,0:T(8,128)(2,1)S(1)} %collective-permute-done.28.refs_18_), channel_id=1, source_target_pairs={{0,1},{1,0},{2,3},{3,2},{4,5},{5,4},{6,7},{7,6},{8,9},{9,8},{10,11... | collective-permute-start | bytes 983048 | tf_op jit(solution)/shard_map/ppermute | solution.py:40
  113.8 17.4 %copy-start.15 = (bf16[2,32,2560]{2,1,0:T(8,128)(2,1)}, bf16[2,32,2560]{2,1,0:T(8,128)(2,1)S(1)}, u32[]{:S(2)}) copy-start(bf16[2,32,2560]{2,1,0:T(8,128)(2,1)S(1)} %collective-permute-done.27.refs_17_) | copy-start | bytes 983044
  113.8 18.1 %collective-permute-start.25 = (bf16[4,32,2560]{2,1,0:T(8,128)(2,1)}, bf16[4,32,2560]{2,1,0:T(8,128)(2,1)}, u32[]{:S(2)}, u32[]{:S(2)}) collective-permute-start(bf16[4,32,2560]{2,1,0:T(8,128)(2,1)} %collective-permute-done.24.refs_14_), channel_id=1, source_target_pairs={{0,1},{1,0},{2,3},{3,2},{4,5},{5,4},{6,7},{7,6},{8,9},{9,8},{10,11... | collective-permute-start | bytes 1966088 | tf_op jit(solution)/shard_map/ppermute | solution.py:40
  124.5 6.7 %copy-start.8 = (bf16[8,16,2560]{2,1,0:T(8,128)(2,1)}, bf16[8,16,2560]{2,1,0:T(8,128)(2,1)S(1)}, u32[]{:S(2)}) copy-start(bf16[8,16,2560]{2,1,0:T(8,128)(2,1)S(1)} %collective-permute-done.14.refs_1_) | copy-start | bytes 1966084
  124.5 23.6 %collective-permute-start.20 = (bf16[4,32,2560]{2,1,0:T(8,128)(2,1)S(1)}, bf16[4,32,2560]{2,1,0:T(8,128)(2,1)}, u32[]{:S(2)}, u32[]{:S(2)}) collective-permute-start(bf16[4,32,2560]{2,1,0:T(8,128)(2,1)S(1)} %slice.51), channel_id=1, source_target_pairs={{0,24},{8,0},{16,8},{24,16},{1,25},{9,1},{17,9},{25,17},{2,26},{10... | collective-permute-start | bytes 1966088 | tf_op jit(solution)/shard_map/ppermute | solution.py:40
  126.3 4.8 %copy-start.9 = (bf16[8,16,2560]{2,1,0:T(8,128)(2,1)}, bf16[8,16,2560]{2,1,0:T(8,128)(2,1)S(1)}, u32[]{:S(2)}) copy-start(bf16[8,16,2560]{2,1,0:T(8,128)(2,1)S(1)} %collective-permute-done.15.refs_2_) | copy-start | bytes 1966084
  126.3 22.4 %collective-permute-start.21 = (bf16[4,32,2560]{2,1,0:T(8,128)(2,1)S(1)}, bf16[4,32,2560]{2,1,0:T(8,128)(2,1)S(1)}, u32[]{:S(2)}, u32[]{:S(2)}) collective-permute-start(bf16[4,32,2560]{2,1,0:T(8,128)(2,1)S(1)} %slice.52), channel_id=1, source_target_pairs={{0,8},{8,16},{16,24},{24,0},{1,9},{9,17},{17,25},{25,1},{2,10},{10... | collective-permute-start | bytes 1966088 | tf_op jit(solution)/shard_map/ppermute | solution.py:40
  129.6 19.1 %copy-start.16 = (bf16[2,32,2560]{2,1,0:T(8,128)(2,1)}, bf16[2,32,2560]{2,1,0:T(8,128)(2,1)S(1)}, u32[]{:S(2)}) copy-start(bf16[2,32,2560]{2,1,0:T(8,128)(2,1)S(1)} %collective-permute-done.29.refs_19_) | copy-start | bytes 983044
  129.6 15.9 %collective-permute-start.16 = (bf16[4,16,2560]{2,1,0:T(8,128)(2,1)S(1)}, bf16[4,16,2560]{2,1,0:T(8,128)(2,1)}, u32[]{:S(2)}, u32[]{:S(2)}) collective-permute-start(bf16[4,16,2560]{2,1,0:T(8,128)(2,1)S(1)} %slice.49), channel_id=1, source_target_pairs={{0,6},{2,0},{4,2},{6,4},{1,7},{3,1},{5,3},{7,5},{8,14},{10,8},{12,... | collective-permute-start | bytes 983048 | tf_op jit(solution)/shard_map/ppermute | solution.py:40
  129.7 1.5 copy-start.11
  129.7 18.3 %collective-permute-start.17 = (bf16[4,16,2560]{2,1,0:T(8,128)(2,1)S(1)}, bf16[4,16,2560]{2,1,0:T(8,128)(2,1)}, u32[]{:S(2)}, u32[]{:S(2)}) collective-permute-start(bf16[4,16,2560]{2,1,0:T(8,128)(2,1)S(1)} %slice.50), channel_id=1, source_target_pairs={{0,2},{2,4},{4,6},{6,0},{1,3},{3,5},{5,7},{7,1},{8,10},{10,12},{12... | collective-permute-start | bytes 983048 | tf_op jit(solution)/shard_map/ppermute | solution.py:40
  148.7 0.8 copy-start.12
  149.5 56.9 %copy-start = (bf16[1,80,2560]{2,1,0:T(8,128)(2,1)S(1)}, bf16[1,80,2560]{2,1,0:T(8,128)(2,1)}, u32[]{:S(2)}) copy-start(bf16[1,80,2560]{2,1,0:T(8,128)(2,1)} %param.17) | copy-start | bytes 1228804
  149.5 56.9 %copy-start.2 = (f32[1,80,2560]{2,1,0:T(8,128)S(1)}, f32[1,80,2560]{2,1,0:T(8,128)}, u32[]{:S(2)}) copy-start(f32[1,80,2560]{2,1,0:T(8,128)} %param.18) | copy-start | bytes 2457604
  199.6 6.9 %collective-permute-start.30 = (bf16[80,2560]{1,0:T(8,128)(2,1)S(1)}, bf16[80,2560]{1,0:T(8,128)(2,1)S(1)}, u32[]{:S(2)}, u32[]{:S(2)}) collective-permute-start(bf16[80,2560]{1,0:T(8,128)(2,1)S(1)} %broadcast_select_fusion), channel_id=1, source_target_pairs={{0,1},{1,0},{2,3},{3,2},{4,5},{5,4},{6,7},{7,6},{8,9},{9,8},{10,11... | collective-permute-start | bytes 1228808 | tf_op jit(solution)/shard_map/ppermute | solution.py:32
  208.8 20.2 %collective-permute-start = (bf16[80,2560]{1,0:T(8,128)(2,1)S(1)}, bf16[80,2560]{1,0:T(8,128)(2,1)}, u32[]{:S(2)}, u32[]{:S(2)}) collective-permute-start(bf16[80,2560]{1,0:T(8,128)(2,1)S(1)} %param), channel_id=1, source_target_pairs={{0,32},{32,0},{64,96},{96,64},{1,33},{33,1},{65,97},{97,65},{2,34}... | collective-permute-start | bytes 1228808 | tf_op jit(solution)/shard_map/cond/branch_0_fun/ppermute | solution.py:32
Sparse Core Ops, SparseCore 0:
  67.4 130.9 reduce-scatter.1

commit v3 on v2

--- a/solution.py
+++ b/solution.py
@@ -35,6 +35,7 @@
 ROWS_A, ROWS_B, ROWS_C = 32, 16, 32
 OFF_A, OFF_B, OFF_C = 0, 32, 48
 
+
 def from_(block, axis, distance):
     count = lax.axis_size(axis)
     return lax.ppermute(block, axis, [(i, (i - distance) % count) for i in range(count)])
@@ -49,46 +50,16 @@
     return up, down, two_low, two_high
 
 
-def direct_gather(block, axis):
-    return jnp.concatenate(
-        [block, from_(block, axis, 1), from_(block, axis, 2), from_(block, axis, -1)], axis=0
-    )
-
-
-def gather_first(shard):
-    a = shard[OFF_A : OFF_A + ROWS_A][None]
-    b = shard[OFF_B : OFF_B + ROWS_B][None]
-    c = shard[OFF_C : OFF_C + ROWS_C][None]
-    b2 = jnp.concatenate([b, from_(b, AY, 1)], axis=0)
-    c2 = jnp.concatenate([c, from_(c, AY, 1)], axis=0)
-    return direct_gather(a, AX), b2, c2
-
-
-def gather_second(a4, b2, c2):
-    return direct_gather(b2, AX), direct_gather(c2, AZ), from_(a4, AY, 1)
-
-
-def gather_last(a4, b8, c8, a4_y):
+def long_parts(b8, c8):
     parts = []
     order = [(dx, dy) for dx in range(4) for dy in range(2)]
-    a_up, a_down, a_low, a_high = ring_gather(a4, AZ)
-    up, down, low, high = ring_gather(b8, AZ)
-    for array, dz, places in ((b8, 0, order), (up, 1, order), (down, 3, order), (low, 2, order[:4]), (high, 2, order[4:])):
+    c_rest = ring_gather(c8, AX)
+    b_rest = ring_gather(b8, AZ)
+    slots = ((0, order), (1, order), (3, order), (2, order[:4]), (2, order[4:]))
+    for array, (dz, places) in zip((b8, *b_rest), slots):
         parts.append((array, OFF_B, [(dx, dz, dy) for dx, dy in places]))
-    up, down, low, high = ring_gather(c8, AX)
-    for array, dx, places in ((c8, 0, order), (up, 1, order), (down, 3, order), (low, 2, order[:4]), (high, 2, order[4:])):
+    for array, (dx, places) in zip((c8, *c_rest), slots):
         parts.append((array, OFF_C, [(dx, dz, dy) for dz, dy in places]))
-    mine = [
-        (a4, a4_y, [(k, 0) for k in range(4)]),
-        (a_up, None, [(k, 1) for k in range(4)]),
-        (a_down, None, [(k, 3) for k in range(4)]),
-        (a_low, None, [(k, 2) for k in range(2)]),
-        (a_high, None, [(k, 2) for k in range(2, 4)]),
-    ]
-    for array, across, places in mine:
-        across = from_(array, AY, 1) if across is None else across
-        parts.append((array, OFF_A, [(dx, dz, 0) for dx, dz in places]))
-        parts.append((across, OFF_A, [(dx, dz, 1) for dx, dz in places]))
     return parts
 
 
@@ -167,8 +138,8 @@
         for part, (off, offsets) in zip(parts, places):
             rows = part.shape[1]
             for slot, (dx, dz, dy) in enumerate(offsets):
-                x = (pos[0] + dx) % 4
-                z = (pos[1] + dz) % 4
+                x = dx if off == OFF_A else (pos[0] + dx) % 4
+                z = dz if off == OFF_A else (pos[1] + dz) % 4
                 y = (pos[2] + dy) % 2
                 row = pl.multiple_of((x * 8 + z * 2 + y) * SHARD + off, 16)
                 copies.append(
@@ -231,14 +202,23 @@
     pos = jnp.stack([lax.axis_index(AX), lax.axis_index(AZ), lax.axis_index(AY)]).astype(jnp.int32)
     doc_col = jnp.broadcast_to(doc_ids[0][:, None], (TOK, HEAD_SIZE))
     doc_row = jnp.broadcast_to(doc_ids, (8, TOK))
-    first = gather_first(shard)
+    a16 = lax.all_gather(shard[OFF_A : OFF_A + ROWS_A], (AX, AZ))
+    bc = shard[OFF_B:]
+    bc2 = jnp.stack([bc, from_(bc, AY, 1)])
     done = forward_pass(q, k, v, og, doc_col, doc_row, 0, 1)
-    first, done = lax.optimization_barrier((first, done))
-    second = gather_second(*first)
-    done = forward_pass(q, k, v, og, doc_col, doc_row, 1, 2, done)
-    second, done = lax.optimization_barrier((second, done))
-    parts = gather_last(first[0], *second)
-    context, term = forward_pass(q, k, v, og, doc_col, doc_row, 3, 1, done)
+    bc2, done = lax.optimization_barrier((bc2, done))
+    b2, c2 = bc2[:, :ROWS_B], bc2[:, ROWS_B:]
+    near = [from_(c2, AZ, 1), from_(c2, AZ, 2), from_(c2, AZ, -1), from_(b2, AX, 1), from_(b2, AX, -1)]
+    done = forward_pass(q, k, v, og, doc_col, doc_row, 1, 1, done)
+    near, b2, c2, done = lax.optimization_barrier((near, b2, c2, done))
+    c8 = jnp.concatenate([c2, *near[:3]], axis=0)
+    b8 = jnp.concatenate([b2, near[3], from_(b2, AX, 2), near[4]], axis=0)
+    context, term = forward_pass(q, k, v, og, doc_col, doc_row, 2, 2, done)
+    places = [(n // 4, n % 4) for n in range(16)]
+    parts = [
+        (a16, OFF_A, [(dx, dz, 0) for dx, dz in places]),
+        (from_(a16, AY, 1), OFF_A, [(dx, dz, 1) for dx, dz in places]),
+    ] + long_parts(b8, c8)
     pair = lax.psum_scatter(term, (AX, AZ), scatter_dimension=0, tiled=True)
     block_out, query_grad, key_grad, value_grad = backward_pass(
         pos, q, k, v, og, context, residual_in[0], doc_col, doc_row, parts

time: 238 us -> 243 us (1.021)
  waiting for transfers between devices: 83.3 us -> 110 us
  starting transfers between devices: 55.6 us -> 32.3 us
  local copies, waits for them, and re-layouts: 6.2 us -> 8.75 us
    ppermute x28 -> x16, waiting for transfers between devices: 70.3 us -> 95 us  [from_(): lax.ppermute(block, axis, [(i, (i - distance) % count) for i in range(cou...]
    ppermute x28 -> x16, starting transfers between devices: 35.5 us -> 17.9 us  [from_(): lax.ppermute(block, axis, [(i, (i - distance) % count) for i in range(cou...]
    all_gather x0 -> x1, waiting for transfers between devices: none -> 7.57 us  [on_device(): a16 = lax.all_gather(shard[OFF_A:OFF_A + ROWS_A], (AX, AZ))]
    reduce_scatter x1, waiting for transfers between devices: 6.65 us -> 0.02 us  [on_device(): pair = lax.psum_scatter(term, (AX, AZ), scatter_dimension=0, tiled=True)]
    ppermute x2, starting transfers between devices: 20.1 us -> 14.2 us  [swapped(): lax.ppermute(block, axis, [(i, i ^ 1 << distance) for i in range(count)])]
  transfers between devices with their start and end apart: 31 -> 20, of which waited for: 14 -> 9; matrix products, arithmetic and copies ran while one was open for 2% -> 3% of each run, Pallas kernels for 26% -> 29%
where the time goes in v3:
time: 243 us
  waiting for transfers between devices  110 us (45%)
  Pallas kernels  69.8 us (29%)
  starting transfers between devices  32.3 us (13%)
  between operations  14.9 us (6%)
  local copies, waits for them, and re-layouts  8.75 us (4%)
  other arithmetic  6.7 us (3%)
    ppermute x16, waiting for transfers between devices, from_(): lax.ppermute(block, axis, [(i, (i - distance) % count) for i in range(cou...  95 us
    pallas_call x1, Pallas kernels, backward_pass(): pl.pallas_call(functools.partial(backward_kernel, places), out_shape=[jax...  41.6 us
    pallas_call x3, Pallas kernels, forward_pass(): pl.pallas_call(forward_kernel, out_shape=[jax.ShapeDtypeStruct((TOK, WIDT...  28.3 us
    ppermute x16, starting transfers between devices, from_(): lax.ppermute(block, axis, [(i, (i - distance) % count) for i in range(cou...  17.9 us
    ppermute x2, starting transfers between devices, swapped(): lax.ppermute(block, axis, [(i, i ^ 1 << distance) for i in range(count)])  14.2 us
    ppermute x2, waiting for transfers between devices, swapped(): lax.ppermute(block, axis, [(i, i ^ 1 << distance) for i in range(count)])  7.63 us
    all_gather x1, waiting for transfers between devices, on_device(): a16 = lax.all_gather(shard[OFF_A:OFF_A + ROWS_A], (AX, AZ))  7.57 us
  transfers between devices with their start and end apart: 20, of which 9 were waited for; matrix products, arithmetic and copies ran while one was open for 3% of the time, Pallas kernels for 29%

profile of v3, /device:TPU:1, one launch (start us, length us, event | category | flops | bytes accessed | tf_op | source)
XLA Modules:
  0.0 242.7 jit_solution(6061739401724508310)
XLA Ops:
  7.2 0.0 all-gather.2.cloned.1.call-start
  7.2 1.6 slice.40
  8.8 0.0 reduce-scatter.2.cloned.1.call-start
  8.9 1.0 fusion.3
  9.9 2.2 collective-permute-start.2
  12.1 0.7 reduce
  12.8 0.8 broadcast_in_dim.31.doc_col
  13.6 0.6 broadcast_in_dim.32.doc_row
  14.2 7.9 %attend_forward.3 = (bf16[384,2560]{1,0:T(8,128)(2,1)}, bf16[2560,2560]{1,0:T(8,128)(2,1)}) custom-call(bf16[384,2560]{1,0:T(8,128)(2,1)} %bitcast.32, bf16[384,2560]{1,0:T(8,128)(2,1)} %bitcast.36, bf16[384,2560]{1,0:T(8,128)(2,1)} %bitcast.40, bf16[384,2560]{1,0:T(8,128)(2,1)} %bitcast.44, s32[384,128]{1,0:T(8,128)} %broadcast_in_dim.31.doc_col, ...), custom_call_target="tpu_custom_call" | custom-call | flops 1650000000 | bytes 6000000 | tf_op jit(solution)/shard_map/attend_forward/pallas_call | solution.py:105
  22.1 3.8 %collective-permute-start.3 = (bf16[2,32,2560]{2,1,0:T(8,128)(2,1)S(1)}, bf16[2,32,2560]{2,1,0:T(8,128)(2,1)S(1)}, u32[]{:S(2)}, u32[]{:S(2)}) collective-permute-start(bf16[2,32,2560]{2,1,0:T(8,128)(2,1)S(1)} %slice.38), channel_id=1, source_target_pairs={{0,6},{2,0},{4,2},{6,4},{1,7},{3,1},{5,3},{7,5},{8,14},{10,8},{12,... | collective-permute-start | bytes 983048 | tf_op jit(solution)/shard_map/ppermute | solution.py:41
  26.0 0.7 collective-permute-start.5
  26.7 2.5 %collective-permute-start.6 = (bf16[2,16,2560]{2,1,0:T(8,128)(2,1)S(1)}, bf16[2,16,2560]{2,1,0:T(8,128)(2,1)S(1)}, u32[]{:S(2)}, u32[]{:S(2)}) collective-permute-start(bf16[2,16,2560]{2,1,0:T(8,128)(2,1)S(1)} %slice.39), channel_id=1, source_target_pairs={{0,24},{8,0},{16,8},{24,16},{1,25},{9,1},{17,9},{25,17},{2,26},{10... | collective-permute-start | bytes 491528 | tf_op jit(solution)/shard_map/ppermute | solution.py:41
  29.2 7.9 %attend_forward.4 = (bf16[384,2560]{1,0:T(8,128)(2,1)}, bf16[2560,2560]{1,0:T(8,128)(2,1)}) custom-call(bf16[384,2560]{1,0:T(8,128)(2,1)} %bitcast.33, bf16[384,2560]{1,0:T(8,128)(2,1)} %bitcast.37, bf16[384,2560]{1,0:T(8,128)(2,1)} %bitcast.41, bf16[384,2560]{1,0:T(8,128)(2,1)} %bitcast.45, ...), custom_call_target="tpu_custom_call", output_to_operand_aliasing={{0}: (6, {}), {1}: (7, {})} | custom-call | flops 1650000000 | bytes 6000000 | tf_op jit(solution)/shard_map/attend_forward/pallas_call | solution.py:105
  37.2 8.0 %collective-permute-done.5 = bf16[2,32,2560]{2,1,0:T(8,128)(2,1)S(1)} collective-permute-done((bf16[2,32,2560]{2,1,0:T(8,128)(2,1)S(1)}, bf16[2,32,2560]{2,1,0:T(8,128)(2,1)S(1)}, u32[]{:S(2)}, u32[]{:S(2)}) %collective-permute-start.5) | collective-permute-done | bytes 327712 | tf_op jit(solution)/shard_map/ppermute | solution.py:41
  45.2 12.5 %attend_forward.5 = (bf16[384,2560]{1,0:T(8,128)(2,1)}, bf16[2560,2560]{1,0:T(8,128)(2,1)}) custom-call(bf16[384,2560]{1,0:T(8,128)(2,1)} %bitcast.34, bf16[384,2560]{1,0:T(8,128)(2,1)} %bitcast.38, bf16[384,2560]{1,0:T(8,128)(2,1)} %bitcast.42, bf16[384,2560]{1,0:T(8,128)(2,1)} %bitcast.46, ...), custom_call_target="tpu_custom_call", output_to_operand_aliasing={{0}: (6, {}), {1}: (7, {})} | custom-call | flops 3300000000 | bytes 12000000 | tf_op jit(solution)/shard_map/attend_forward/pallas_call | solution.py:105
  57.7 0.8 constant_dynamic-update-slice_fusion.7
  58.5 0.8 constant_dynamic-update-slice_fusion.6
  59.3 0.7 constant_dynamic-update-slice_fusion.5
  60.0 7.6 %all-gather.2.cloned.1.call-done.refs_0_ = bf16[16,32,2560]{2,1,0:T(8,128)(2,1)} async-done(((bf16[1,32,2560]{2,1,0:T(8,128)(2,1)}), bf16[16,32,2560]{2,1,0:T(8,128)(2,1)}) %all-gather.2.cloned.1.call-update) | async-done | bytes 2621456 | tf_op jit(solution)/shard_map/all_gather | solution.py:205
  67.6 1.2 collective-permute-start.8
  68.8 0.7 constant_dynamic-update-slice_fusion.4.refs_7_
  69.5 1.2 collective-permute-start.14
  70.7 0.2 collective-permute-start.15
  71.0 1.2 collective-permute-start.9
  72.2 49.6 %collective-permute-done.9 = bf16[2,16,2560]{2,1,0:T(8,128)(2,1)S(1)} collective-permute-done((bf16[2,16,2560]{2,1,0:T(8,128)(2,1)S(1)}, bf16[2,16,2560]{2,1,0:T(8,128)(2,1)S(1)}, u32[]{:S(2)}, u32[]{:S(2)}) %collective-permute-start.9) | collective-permute-done | bytes 163872 | tf_op jit(solution)/shard_map/ppermute | solution.py:41
  121.8 0.9 collective-permute-start.10
  122.8 0.6 collective-permute-start.11
  123.4 2.8 %collective-permute-start.16 = (bf16[4,32,2560]{2,1,0:T(8,128)(2,1)S(1)}, bf16[4,32,2560]{2,1,0:T(8,128)(2,1)S(1)}, u32[]{:S(2)}, u32[]{:S(2)}) collective-permute-start(bf16[4,32,2560]{2,1,0:T(8,128)(2,1)S(1)} %slice.49), channel_id=1, source_target_pairs={{0,24},{8,0},{16,8},{24,16},{1,25},{9,1},{17,9},{25,17},{2,26},{10... | collective-permute-start | bytes 1966088 | tf_op jit(solution)/shard_map/ppermute | solution.py:41
  126.3 0.1 collective-permute-start.17
  126.3 19.5 %collective-permute-done.10.refs_3_ = bf16[8,16,2560]{2,1,0:T(8,128)(2,1)S(1)} collective-permute-done((bf16[8,16,2560]{2,1,0:T(8,128)(2,1)S(1)}, bf16[8,16,2560]{2,1,0:T(8,128)(2,1)S(1)}, u32[]{:S(2)}, u32[]{:S(2)}) %collective-permute-start.10) | collective-permute-done | bytes 655392 | tf_op jit(solution)/shard_map/ppermute | solution.py:41
  145.9 0.1 collective-permute-start.12
  145.9 1.9 collective-permute-done.11.refs_4_
  147.9 0.3 collective-permute-start.13
  148.2 0.5 copy-done.5
  148.7 0.6 pad_add_fusion.pos
  149.3 13.0 %collective-permute-done.12.refs_5_ = bf16[4,16,2560]{2,1,0:T(8,128)(2,1)} collective-permute-done((bf16[4,16,2560]{2,1,0:T(8,128)(2,1)S(1)}, bf16[4,16,2560]{2,1,0:T(8,128)(2,1)}, u32[]{:S(2)}, u32[]{:S(2)}) %collective-permute-start.12) | collective-permute-done | bytes 327712 | tf_op jit(solution)/shard_map/ppermute | solution.py:41
  162.3 3.0 %collective-permute-done.13.refs_6_ = bf16[4,16,2560]{2,1,0:T(8,128)(2,1)} collective-permute-done((bf16[4,16,2560]{2,1,0:T(8,128)(2,1)S(1)}, bf16[4,16,2560]{2,1,0:T(8,128)(2,1)}, u32[]{:S(2)}, u32[]{:S(2)}) %collective-permute-start.13) | collective-permute-done | bytes 327712 | tf_op jit(solution)/shard_map/ppermute | solution.py:41
  165.3 0.8 copy-done.7
  166.2 0.2 copy-done.8
  166.4 41.6 %attend_backward.1 = (bf16[384,2560]{1,0:T(8,128)(2,1)}, bf16[384,2560]{1,0:T(8,128)(2,1)}, bf16[384,2560]{1,0:T(8,128)(2,1)}, bf16[384,2560]{1,0:T(8,128)(2,1)}) custom-call(s32[3]{0:T(128)} %pad_add_fusion.pos, bf16[384,2560]{1,0:T(8,128)(2,1)} %bitcast.35, bf16[384,2560]{1,0:T(8,128)(2,1)} %bitcast.39, bf16[384,2560]{1,0:T(8,128)(2,1)} %bitcast.43, ...), custom_call_target="tpu_custom_call" | custom-call | flops 14000000000 | bytes 35000000 | tf_op jit(solution)/shard_map/attend_backward/pallas_call | solution.py:174
  208.0 1.2 broadcast_select_fusion
  209.1 0.1 collective-permute-start.18
  209.9 6.1 %collective-permute-done.18 = bf16[80,2560]{1,0:T(8,128)(2,1)S(1)} collective-permute-done((bf16[80,2560]{1,0:T(8,128)(2,1)S(1)}, bf16[80,2560]{1,0:T(8,128)(2,1)S(1)}, u32[]{:S(2)}, u32[]{:S(2)}) %collective-permute-start.18) | collective-permute-done | bytes 409632 | tf_op jit(solution)/shard_map/ppermute | solution.py:32
  216.0 2.3 fusion.2
  218.3 15.7 %conditional.4 = (bf16[80,2560]{1,0:T(8,128)(2,1)}) conditional(s32[]{:T(128)} %clamp.3, bf16[80,2560]{1,0:T(8,128)(2,1)S(1)} %get-tuple-element.66, bf16[80,2560]{1,0:T(8,128)(2,1)S(1)} %get-tuple-element.66), branch_computations={%region_1.2_spmd, %region_2.3_spmd} | conditional | bytes 1638448
  218.3 14.2 %collective-permute-start = (bf16[80,2560]{1,0:T(8,128)(2,1)S(1)}, bf16[80,2560]{1,0:T(8,128)(2,1)}, u32[]{:S(2)}, u32[]{:S(2)}) collective-permute-start(bf16[80,2560]{1,0:T(8,128)(2,1)S(1)} %param), channel_id=1, source_target_pairs={{0,32},{32,0},{64,96},{96,64},{1,33},{33,1},{65,97},{97,65},{2,34}... | collective-permute-start | bytes 1228808 | tf_op jit(solution)/shard_map/cond/branch_0_fun/ppermute | solution.py:32
  232.5 1.5 collective-permute-done
  234.0 1.9 fusion.1
  (41 shorter events, 0.4 us)
Async XLA Ops:
  7.2 60.4 %all-gather.2.cloned.1.call-start = ((), (), s32[]{:S(2)}) async-start(), calls=%async_computation.1 | async-start | bytes 2785280 | tf_op jit(solution)/shard_map/all_gather | solution.py:205
  8.8 199.1 %reduce-scatter.2.cloned.1.call-start = ((), (), s32[]{:S(2)}) async-start(), calls=%async_computation.2 | async-start | bytes 13926400 | tf_op jit(solution)/shard_map/reduce_scatter | solution.py:222
  9.9 12.2 %collective-permute-start.2 = (bf16[48,2560]{1,0:T(8,128)(2,1)S(1)}, bf16[48,2560]{1,0:T(8,128)(2,1)S(1)}, u32[]{:S(2)}, u32[]{:S(2)}) collective-permute-start(bf16[48,2560]{1,0:T(8,128)(2,1)S(1)} %get-tuple-element.68), channel_id=1, source_target_pairs={{0,1},{1,0},{2,3},{3,2},{4,5},{5,4},{6,7},{7,6},{8,9},{9,8},{10,11... | collective-permute-start | bytes 737288 | tf_op jit(solution)/shard_map/ppermute | solution.py:41
  22.1 15.1 %collective-permute-start.3 = (bf16[2,32,2560]{2,1,0:T(8,128)(2,1)S(1)}, bf16[2,32,2560]{2,1,0:T(8,128)(2,1)S(1)}, u32[]{:S(2)}, u32[]{:S(2)}) collective-permute-start(bf16[2,32,2560]{2,1,0:T(8,128)(2,1)S(1)} %slice.38), channel_id=1, source_target_pairs={{0,6},{2,0},{4,2},{6,4},{1,7},{3,1},{5,3},{7,5},{8,14},{10,8},{12,... | collective-permute-start | bytes 983048 | tf_op jit(solution)/shard_map/ppermute | solution.py:41
  26.0 11.2 %collective-permute-start.4 = (bf16[2,32,2560]{2,1,0:T(8,128)(2,1)S(1)}, bf16[2,32,2560]{2,1,0:T(8,128)(2,1)S(1)}, u32[]{:S(2)}, u32[]{:S(2)}) collective-permute-start(bf16[2,32,2560]{2,1,0:T(8,128)(2,1)S(1)} %slice.38), channel_id=1, source_target_pairs={{0,4},{2,6},{4,0},{6,2},{1,5},{3,7},{5,1},{7,3},{8,12},{10,14},{12... | collective-permute-start | bytes 983048 | tf_op jit(solution)/shard_map/ppermute | solution.py:41
  26.0 19.3 %collective-permute-start.5 = (bf16[2,32,2560]{2,1,0:T(8,128)(2,1)S(1)}, bf16[2,32,2560]{2,1,0:T(8,128)(2,1)S(1)}, u32[]{:S(2)}, u32[]{:S(2)}) collective-permute-start(bf16[2,32,2560]{2,1,0:T(8,128)(2,1)S(1)} %slice.38), channel_id=1, source_target_pairs={{0,2},{2,4},{4,6},{6,0},{1,3},{3,5},{5,7},{7,1},{8,10},{10,12},{12... | collective-permute-start | bytes 983048 | tf_op jit(solution)/shard_map/ppermute | solution.py:41
  26.7 10.5 %collective-permute-start.6 = (bf16[2,16,2560]{2,1,0:T(8,128)(2,1)S(1)}, bf16[2,16,2560]{2,1,0:T(8,128)(2,1)S(1)}, u32[]{:S(2)}, u32[]{:S(2)}) collective-permute-start(bf16[2,16,2560]{2,1,0:T(8,128)(2,1)S(1)} %slice.39), channel_id=1, source_target_pairs={{0,24},{8,0},{16,8},{24,16},{1,25},{9,1},{17,9},{25,17},{2,26},{10... | collective-permute-start | bytes 491528 | tf_op jit(solution)/shard_map/ppermute | solution.py:41
  29.2 8.0 %collective-permute-start.7 = (bf16[2,16,2560]{2,1,0:T(8,128)(2,1)S(1)}, bf16[2,16,2560]{2,1,0:T(8,128)(2,1)S(1)}, u32[]{:S(2)}, u32[]{:S(2)}) collective-permute-start(bf16[2,16,2560]{2,1,0:T(8,128)(2,1)S(1)} %slice.39), channel_id=1, source_target_pairs={{0,8},{8,16},{16,24},{24,0},{1,9},{9,17},{17,25},{25,1},{2,10},{10... | collective-permute-start | bytes 491528 | tf_op jit(solution)/shard_map/ppermute | solution.py:41
  67.6 97.8 %collective-permute-start.8 = (bf16[16,32,2560]{2,1,0:T(8,128)(2,1)}, bf16[16,32,2560]{2,1,0:T(8,128)(2,1)}, u32[]{:S(2)}, u32[]{:S(2)}) collective-permute-start(bf16[16,32,2560]{2,1,0:T(8,128)(2,1)} %all-gather.2.cloned.1.call-done.refs_0_), channel_id=1, source_target_pairs={{0,1},{1,0},{2,3},{3,2},{4,5},{5,4},{6,7},{7,6},{8,9},{9,8},{10,11... | collective-permute-start | bytes 7864328 | tf_op jit(solution)/shard_map/ppermute | solution.py:41
  69.5 53.8 %collective-permute-start.14 = (bf16[8,32,2560]{2,1,0:T(8,128)(2,1)}, bf16[8,32,2560]{2,1,0:T(8,128)(2,1)S(1)}, u32[]{:S(2)}, u32[]{:S(2)}) collective-permute-start(bf16[8,32,2560]{2,1,0:T(8,128)(2,1)} %constant_dynamic-update-slice_fusion.4.refs_7_), channel_id=1, source_target_pairs={{0,24},{8,0},{16,8},{24,16},{1,25},{9,1},{17,9},{25,17},{2,26},{10... | collective-permute-start | bytes 3932168 | tf_op jit(solution)/shard_map/ppermute | solution.py:41
  70.7 55.5 %collective-permute-start.15 = (bf16[8,32,2560]{2,1,0:T(8,128)(2,1)}, bf16[8,32,2560]{2,1,0:T(8,128)(2,1)S(1)}, u32[]{:S(2)}, u32[]{:S(2)}) collective-permute-start(bf16[8,32,2560]{2,1,0:T(8,128)(2,1)} %constant_dynamic-update-slice_fusion.4.refs_7_), channel_id=1, source_target_pairs={{0,8},{8,16},{16,24},{24,0},{1,9},{9,17},{17,25},{25,1},{2,10},{10... | collective-permute-start | bytes 3932168 | tf_op jit(solution)/shard_map/ppermute | solution.py:41
  71.0 50.8 %collective-permute-start.9 = (bf16[2,16,2560]{2,1,0:T(8,128)(2,1)S(1)}, bf16[2,16,2560]{2,1,0:T(8,128)(2,1)S(1)}, u32[]{:S(2)}, u32[]{:S(2)}) collective-permute-start(bf16[2,16,2560]{2,1,0:T(8,128)(2,1)S(1)} %slice.39), channel_id=1, source_target_pairs={{0,16},{8,24},{16,0},{24,8},{1,17},{9,25},{17,1},{25,9},{2,18},{10... | collective-permute-start | bytes 491528 | tf_op jit(solution)/shard_map/ppermute | solution.py:41
  121.8 26.4 %copy-start.6 = (bf16[8,16,2560]{2,1,0:T(8,128)(2,1)}, bf16[8,16,2560]{2,1,0:T(8,128)(2,1)S(1)}, u32[]{:S(2)}) copy-start(bf16[8,16,2560]{2,1,0:T(8,128)(2,1)S(1)} %constant_dynamic-update-slice_fusion.refs_2_) | copy-start | bytes 1966084
  121.8 24.0 %collective-permute-start.10 = (bf16[8,16,2560]{2,1,0:T(8,128)(2,1)S(1)}, bf16[8,16,2560]{2,1,0:T(8,128)(2,1)S(1)}, u32[]{:S(2)}, u32[]{:S(2)}) collective-permute-start(bf16[8,16,2560]{2,1,0:T(8,128)(2,1)S(1)} %constant_dynamic-update-slice_fusion.refs_2_), channel_id=1, source_target_pairs={{0,6},{2,0},{4,2},{6,4},{1,7},{3,1},{5,3},{7,5},{8,14},{10,8},{12,... | collective-permute-start | bytes 1966088 | tf_op jit(solution)/shard_map/ppermute | solution.py:41
  122.8 25.1 %collective-permute-start.11 = (bf16[8,16,2560]{2,1,0:T(8,128)(2,1)S(1)}, bf16[8,16,2560]{2,1,0:T(8,128)(2,1)S(1)}, u32[]{:S(2)}, u32[]{:S(2)}) collective-permute-start(bf16[8,16,2560]{2,1,0:T(8,128)(2,1)S(1)} %constant_dynamic-update-slice_fusion.refs_2_), channel_id=1, source_target_pairs={{0,2},{2,4},{4,6},{6,0},{1,3},{3,5},{5,7},{7,1},{8,10},{10,12},{12... | collective-permute-start | bytes 1966088 | tf_op jit(solution)/shard_map/ppermute | solution.py:41
  123.4 24.5 %copy-start.2 = (bf16[8,32,2560]{2,1,0:T(8,128)(2,1)}, bf16[8,32,2560]{2,1,0:T(8,128)(2,1)S(1)}, u32[]{:S(2)}) copy-start(bf16[8,32,2560]{2,1,0:T(8,128)(2,1)S(1)} %collective-permute-done.14.refs_8_) | copy-start | bytes 3932164
  123.4 41.9 %collective-permute-start.16 = (bf16[4,32,2560]{2,1,0:T(8,128)(2,1)S(1)}, bf16[4,32,2560]{2,1,0:T(8,128)(2,1)S(1)}, u32[]{:S(2)}, u32[]{:S(2)}) collective-permute-start(bf16[4,32,2560]{2,1,0:T(8,128)(2,1)S(1)} %slice.49), channel_id=1, source_target_pairs={{0,24},{8,0},{16,8},{24,16},{1,25},{9,1},{17,9},{25,17},{2,26},{10... | collective-permute-start | bytes 1966088 | tf_op jit(solution)/shard_map/ppermute | solution.py:41
  126.2 22.0 %copy-start.3 = (bf16[8,32,2560]{2,1,0:T(8,128)(2,1)}, bf16[8,32,2560]{2,1,0:T(8,128)(2,1)S(1)}, u32[]{:S(2)}) copy-start(bf16[8,32,2560]{2,1,0:T(8,128)(2,1)S(1)} %collective-permute-done.15.refs_9_) | copy-start | bytes 3932164
  126.3 39.0 %collective-permute-start.17 = (bf16[4,32,2560]{2,1,0:T(8,128)(2,1)S(1)}, bf16[4,32,2560]{2,1,0:T(8,128)(2,1)S(1)}, u32[]{:S(2)}, u32[]{:S(2)}) collective-permute-start(bf16[4,32,2560]{2,1,0:T(8,128)(2,1)S(1)} %slice.50), channel_id=1, source_target_pairs={{0,8},{8,16},{16,24},{24,0},{1,9},{9,17},{17,25},{25,1},{2,10},{10... | collective-permute-start | bytes 1966088 | tf_op jit(solution)/shard_map/ppermute | solution.py:41
  145.8 2.4 copy-start.4
  145.9 16.5 %collective-permute-start.12 = (bf16[4,16,2560]{2,1,0:T(8,128)(2,1)S(1)}, bf16[4,16,2560]{2,1,0:T(8,128)(2,1)}, u32[]{:S(2)}, u32[]{:S(2)}) collective-permute-start(bf16[4,16,2560]{2,1,0:T(8,128)(2,1)S(1)} %slice.47), channel_id=1, source_target_pairs={{0,6},{2,0},{4,2},{6,4},{1,7},{3,1},{5,3},{7,5},{8,14},{10,8},{12,... | collective-permute-start | bytes 983048 | tf_op jit(solution)/shard_map/ppermute | solution.py:41
  147.8 0.8 copy-start.5
  147.9 17.4 %collective-permute-start.13 = (bf16[4,16,2560]{2,1,0:T(8,128)(2,1)S(1)}, bf16[4,16,2560]{2,1,0:T(8,128)(2,1)}, u32[]{:S(2)}, u32[]{:S(2)}) collective-permute-start(bf16[4,16,2560]{2,1,0:T(8,128)(2,1)S(1)} %slice.48), channel_id=1, source_target_pairs={{0,2},{2,4},{4,6},{6,0},{1,3},{3,5},{5,7},{7,1},{8,10},{10,12},{12... | collective-permute-start | bytes 983048 | tf_op jit(solution)/shard_map/ppermute | solution.py:41
  165.3 0.9 copy-start.7
  165.3 1.1 copy-start.8
  166.4 49.7 %copy-start = (bf16[1,80,2560]{2,1,0:T(8,128)(2,1)S(1)}, bf16[1,80,2560]{2,1,0:T(8,128)(2,1)}, u32[]{:S(2)}) copy-start(bf16[1,80,2560]{2,1,0:T(8,128)(2,1)} %param.17) | copy-start | bytes 1228804
  166.4 49.7 %copy-start.1 = (f32[1,80,2560]{2,1,0:T(8,128)S(1)}, f32[1,80,2560]{2,1,0:T(8,128)}, u32[]{:S(2)}) copy-start(f32[1,80,2560]{2,1,0:T(8,128)} %param.18) | copy-start | bytes 2457604
  209.1 6.9 %collective-permute-start.18 = (bf16[80,2560]{1,0:T(8,128)(2,1)S(1)}, bf16[80,2560]{1,0:T(8,128)(2,1)S(1)}, u32[]{:S(2)}, u32[]{:S(2)}) collective-permute-start(bf16[80,2560]{1,0:T(8,128)(2,1)S(1)} %broadcast_select_fusion), channel_id=1, source_target_pairs={{0,1},{1,0},{2,3},{3,2},{4,5},{5,4},{6,7},{7,6},{8,9},{9,8},{10,11... | collective-permute-start | bytes 1228808 | tf_op jit(solution)/shard_map/ppermute | solution.py:32
  218.3 15.7 %collective-permute-start = (bf16[80,2560]{1,0:T(8,128)(2,1)S(1)}, bf16[80,2560]{1,0:T(8,128)(2,1)}, u32[]{:S(2)}, u32[]{:S(2)}) collective-permute-start(bf16[80,2560]{1,0:T(8,128)(2,1)S(1)} %param), channel_id=1, source_target_pairs={{0,32},{32,0},{64,96},{96,64},{1,33},{33,1},{65,97},{97,65},{2,34}... | collective-permute-start | bytes 1228808 | tf_op jit(solution)/shard_map/cond/branch_0_fun/ppermute | solution.py:32
Sparse Core Ops, SparseCore 0:
  10.8 56.7 all-gather.1
  71.0 130.8 reduce-scatter.1
